TPU v7x, 128 devices: a whole 4x4x4 slice. The times are simulated.
128 devices in a mesh: wide: 16 (over x, z_lo, core), narrow: 8 (over z_hi, y).
Axes of the slice: x: 4, y: 4, z: 4 (z_hi: 2, z_lo: 2; z = z_hi * 2 + z_lo), core: 2. Of those that a mesh axis runs over, the one named last changes fastest.
Arguments:
- amplitudes: float32 [2, 16, 8, 16, 256, 256], P(None, 'wide', 'narrow'), may hold values from -6 to 6
- low_gate: float32 [2, 256, 256], replicated, may hold values from -0.25 to 0.25
- mid_gate: float32 [2, 256, 256], replicated, may hold values from -0.25 to 0.25
- pair_gates: float32 [3, 2, 4, 4], replicated, may hold values from -2 to 2
Outputs:
- remapped: float32 [2, 16, 8, 16, 256, 256], P(None, 'wide', 'narrow')
All inputs are finite; a program needn't handle non-finite values.
Results may differ from a plain program's by a relative error of at most 0.00007.
Values sent between devices are 32-bit elements; how exact they have to be, the bound alone decides.
No kernel may reach another device: no remote copies, remote signals or barrier semaphores. Data moves between devices by JAX's collectives and lax.ppermute only.
A program may use at most 128 MiB of HBM per device.

v0:
```python
import jax
import jax.numpy as jnp
from jax import lax
from jax.sharding import PartitionSpec as P

highest = lax.Precision.HIGHEST


def swapped(x, axis, bit):
    return lax.ppermute(x, axis, [(i, i ^ 1 << bit) for i in range(lax.axis_size(axis))])


def apply_merged(amplitudes, low_gate, mid_gate):
    real_part, imag_part = (amplitudes[0], amplitudes[1])
    low_real, low_imag = (low_gate[0], low_gate[1])
    first_real = jnp.einsum("abhml,il->abhmi", real_part, low_real, precision=highest) - jnp.einsum(
        "abhml,il->abhmi", imag_part, low_imag, precision=highest
    )
    first_imag = jnp.einsum("abhml,il->abhmi", real_part, low_imag, precision=highest) + jnp.einsum(
        "abhml,il->abhmi", imag_part, low_real, precision=highest
    )
    mid_real, mid_imag = (mid_gate[0], mid_gate[1])
    second_real = jnp.einsum(
        "abhml,im->abhil", first_real, mid_real, precision=highest
    ) - jnp.einsum("abhml,im->abhil", first_imag, mid_imag, precision=highest)
    second_imag = jnp.einsum(
        "abhml,im->abhil", first_real, mid_imag, precision=highest
    ) + jnp.einsum("abhml,im->abhil", first_imag, mid_real, precision=highest)
    return jnp.stack([second_real, second_imag])


def partner_gate(state, other, gate, mine, half_bit):
    rows = lax.dynamic_slice_in_dim(gate, 2 * mine, 2, 1)
    own_cols = lax.dynamic_slice_in_dim(rows, 2 * mine, 2, 2)
    far_cols = lax.dynamic_slice_in_dim(rows, 2 - 2 * mine, 2, 2)
    shape = state.shape
    split_shape = shape[:3] + (shape[3] >> half_bit + 1, 2, 1 << half_bit) + shape[4:]
    own_split = state.reshape(split_shape)
    far_split = other.reshape(split_shape)
    outputs = []
    for target in range(2):
        total_real = jnp.zeros(own_split[0, :, :, :, 0].shape, jnp.float32)
        total_imag = jnp.zeros(own_split[0, :, :, :, 0].shape, jnp.float32)
        for source in range(2):
            for coeffs, piece in ((own_cols, own_split), (far_cols, far_split)):
                amplitude = piece[:, :, :, :, source]
                coef_real = coeffs[0, target, source]
                coef_imag = coeffs[1, target, source]
                total_real = total_real + coef_real * amplitude[0] - coef_imag * amplitude[1]
                total_imag = total_imag + coef_real * amplitude[1] + coef_imag * amplitude[0]
        outputs.append(jnp.stack([total_real, total_imag]))
    return jnp.stack(outputs, axis=4).reshape(shape)


def narrow_gate(state, gate):
    other = swapped(state, "narrow", 1)
    mine = lax.axis_index("narrow") >> 1 & 1
    return partner_gate(state, other, gate, mine, 0)


def remap_qubits(state):
    return lax.all_to_all(state, "wide", split_axis=4, concat_axis=4, tiled=True)


def body(amplitudes, low_gate, mid_gate, pair_gates):
    state = apply_merged(amplitudes, low_gate, mid_gate)
    wide_index = lax.axis_index("wide")
    other = swapped(state, "wide", 0)
    state = partner_gate(state, other, pair_gates[0], wide_index & 1, 0)
    other = swapped(state, "wide", 2)
    state = partner_gate(state, other, pair_gates[1], wide_index >> 2 & 1, 1)
    state = narrow_gate(state, pair_gates[2])
    state = remap_qubits(state)
    return state


def solution(mesh):
    in_specs = (P(None, "wide", "narrow", None, None, None), P(), P(), P())
    out_specs = P(None, "wide", "narrow", None, None, None)
    return jax.shard_map(body, mesh=mesh, in_specs=in_specs, out_specs=out_specs, check_vma=False)
```

profile of v0, /device:TPU:1, one launch (start us, length us, event | category | flops | bytes accessed | tf_op | source)
XLA Modules:
  0.0 675.3 jit_solution(6235137157490432231)
XLA Ops:
  0.0 5.5 fusion.2
  5.5 4.5 fusion
  10.0 3.5 fusion.12
  13.5 7.0 %fusion.42 = f32[16,256,256]{2,1,0:T(8,128)S(1)} fusion(f32[16,256,256]{2,1,0:T(8,128)S(1)} %fusion.12, f32[2,256,256]{2,1,0:T(8,128)S(1)} %copy-done.11), kind=kOutput, calls=%fused_computation.77 | convolution fusion | flops 3221225472 | bytes 8650752 | tf_op jit(solution)/shard_map/abhml,im->abhil/dot_general | solution.py:26
  20.5 7.0 %fusion.46 = f32[16,256,256]{2,1,0:T(8,128)S(1)} fusion(f32[16,256,256]{2,1,0:T(8,128)S(1)} %fusion.12, f32[2,256,256]{2,1,0:T(8,128)S(1)} %copy-done.11), kind=kOutput, calls=%fused_computation.81 | convolution fusion | flops 3221225472 | bytes 8650752 | tf_op jit(solution)/shard_map/abhml,im->abhil/dot_general | solution.py:23
  27.5 3.6 fusion.15
  31.1 7.1 %convolution_add_fusion = f32[16,256,256]{2,1,0:T(8,128)S(1)} fusion(f32[16,256,256]{2,1,0:T(8,128)S(1)} %fusion.42, f32[16,256,256]{2,1,0:T(8,128)S(1)} %fusion.15, f32[2,256,256]{2,1,0:T(8,128)S(1)} %copy-done.11), kind=kOutput, calls=%fused_computation.25 | convolution fusion | flops 3222274048 | bytes 12845056 | tf_op jit(solution)/shard_map/abhml,im->abhil/dot_general | solution.py:28
  38.2 7.5 %convolution_subtract_fusion = f32[16,256,256]{2,1,0:T(8,128)S(1)} fusion(f32[16,256,256]{2,1,0:T(8,128)S(1)} %fusion.46, f32[16,256,256]{2,1,0:T(8,128)S(1)} %fusion.15, f32[2,256,256]{2,1,0:T(8,128)S(1)} %copy-done.11), kind=kOutput, calls=%fused_computation.26 | convolution fusion | flops 3222274048 | bytes 12845056 | tf_op jit(solution)/shard_map/abhml,im->abhil/dot_general | solution.py:25
  45.7 4.3 pad_maximum_fusion
  50.2 1.4 collective-permute-start
  51.6 4.6 fusion.62
  56.2 1.9 copy.186
  58.1 4.6 fusion.63
  62.7 2.9 copy.185
  65.7 2.9 copy.182
  68.6 2.9 copy.181
  71.6 0.7 fusion.70
  72.9 6.9 %fusion.61 = (f32[1,1,1,8,1,1,256,256]{6,7,4,3,0,5,2,1:T(8,128)}, f32[1,1,1,8,1,1,256,256]{6,7,4,3,0,5,2,1:T(8,128)}, f32[1,1,1,8,1,1,256,256]{6,7,4,3,0,5,2,1:T(8,128)}, f32[1,1,1,8,1,1,256,256]{6,7,4,3,0,5,2,1:T(8,128)}) fusion(f32[2,1,1,8,2,1,256,256]{6,7,4,3,0,5,2,1:T(8,128)} %bitcast.33), kind=kLoop, calls=%fused_computation.102 | loop fusion | bytes 16777216 | tf_op jit(solution)/shard_map/slice | solution.py:49
  79.8 2.9 copy.188
  82.7 2.9 copy.187
  85.6 2.9 copy.184
  88.5 2.9 copy.183
  91.4 11.9 %add_subtract_fusion = (f32[1,1,1,8,1,1,256,256]{7,6,3,5,4,2,1,0:T(8,128)S(1)}, f32[1,1,1,8,1,1,256,256]{7,6,3,5,4,2,1,0:T(8,128)S(1)}) fusion(f32[1,1,1,8,1,1,256,256]{7,6,3,5,4,2,1,0:T(8,128)} %copy.188, f32[1,1,1,8,1,1,256,256]{7,6,3,5,4,2,1,0:T(8,128)} %copy.187, f32[1,1,1,8,1,1,256,256]{7,6,3,5,4,2,1,0:T(8,128)S(1)} %copy.186, ...), kind=kLoop, calls=%fused_computation.74 | loop fusion | flops 15728640 | bytes 20971552 | tf_op jit(solution)/shard_map/sub | solution.py:49
  103.8 1.1 copy-done.3
  106.8 6.9 %add_subtract_fusion.1 = (f32[1,1,1,8,1,1,256,256]{7,6,3,5,4,2,1,0:T(8,128)S(1)}, f32[1,1,1,8,1,1,256,256]{7,6,3,5,4,2,1,0:T(8,128)S(1)}) fusion(f32[1,1,1,8,1,1,256,256]{7,6,3,5,4,2,1,0:T(8,128)S(1)} %copy-done.6, f32[1,1,1,8,1,1,256,256]{7,6,3,5,4,2,1,0:T(8,128)S(1)} %copy-done.7, f32[1,1,1,8,1,1,256,256]{7,6,3,5,4,2,1,0:T(8,128)S(1)} %copy.186, ...), kind=kLoop, calls=%fused_computation.76 | loop fusion | flops 15728640 | bytes 20971552 | tf_op jit(solution)/shard_map/sub | solution.py:49
  114.1 4.0 pad_maximum_fusion.1
  118.1 1.3 collective-permute-start.1
  120.0 0.7 fusion.67
  120.7 3.6 maximum_maximum_fusion
  124.3 4.0 fusion.60
  128.3 172.1 %collective-permute-done.1 = f32[2,1,1,16,256,256]{5,4,3,0,2,1:T(8,128)S(1)} collective-permute-done((f32[2,1,1,16,256,256]{5,4,3,0,2,1:T(8,128)}, f32[2,1,1,16,256,256]{5,4,3,0,2,1:T(8,128)S(1)}, u32[]{:S(2)}, u32[]{:S(2)}) %collective-permute-start.1) | collective-permute-done | bytes 8388640 | tf_op jit(solution)/shard_map/ppermute | solution.py:10
  300.4 6.0 fusion.33
  306.3 6.0 fusion.41
  312.3 6.1 fusion.39
  318.4 6.1 fusion.36
  325.1 0.9 pad_maximum_fusion.2
  326.0 4.0 copy.153
  329.9 3.0 collective-permute-start.2
  333.6 179.3 %collective-permute-done.2 = f32[2,1,1,16,256,256]{5,4,3,0,2,1:T(8,128)} collective-permute-done((f32[2,1,1,16,256,256]{5,4,3,0,2,1:T(8,128)}, f32[2,1,1,16,256,256]{5,4,3,0,2,1:T(8,128)}, u32[]{:S(2)}, u32[]{:S(2)}) %collective-permute-start.2) | collective-permute-done | bytes 8388640 | tf_op jit(solution)/shard_map/ppermute | solution.py:10
  513.0 11.5 %fusion.18 = f32[1,1,1,8,1,256,256]{6,5,3,4,2,1,0:T(8,128)S(1)} fusion(f32[2,1,1,8,2,1,256,256]{7,6,4,3,0,5,2,1:T(8,128)} %bitcast.92, f32[2,1,1,8,2,1,256,256]{7,6,4,3,0,5,2,1:T(8,128)} %bitcast.97, f32[]{:T(128)} %bitcast.117, f32[]{:T(128)} %bitcast.116, f32[]{:T(128)} %bitcast.114, f32[]{:T(128)} %bitcast.113, f32[]{:T(128)} %bitcast.112, f32[]{:T(128)} %bitcast.111, ...), kind=kLoop, calls=%fused_computation.38 | loop fusion | flops 7864320 | bytes 18874400 | tf_op jit(solution)/shard_map/add | solution.py:50
  524.5 11.3 %fusion.32 = f32[1,1,1,8,1,256,256]{6,5,3,4,2,1,0:T(8,128)S(1)} fusion(f32[2,1,1,8,2,1,256,256]{7,6,4,3,0,5,2,1:T(8,128)} %bitcast.92, f32[2,1,1,8,2,1,256,256]{7,6,4,3,0,5,2,1:T(8,128)} %bitcast.97, f32[]{:T(128)} %bitcast.117, f32[]{:T(128)} %bitcast.116, f32[]{:T(128)} %bitcast.114, f32[]{:T(128)} %bitcast.113, f32[]{:T(128)} %bitcast.112, f32[]{:T(128)} %bitcast.111, ...), kind=kLoop, calls=%fused_computation.58 | loop fusion | flops 7864320 | bytes 18874400 | tf_op jit(solution)/shard_map/sub | solution.py:49
  535.8 11.3 %fusion.28 = f32[1,1,1,8,1,256,256]{6,5,3,0,4,2,1:T(8,128)S(1)} fusion(f32[2,1,1,8,2,1,256,256]{7,6,4,3,0,5,2,1:T(8,128)} %bitcast.92, f32[2,1,1,8,2,1,256,256]{7,6,4,3,0,5,2,1:T(8,128)} %bitcast.97, f32[]{:T(128)} %bitcast.103, f32[]{:T(128)} %bitcast.102, f32[]{:T(128)} %bitcast.100, f32[]{:T(128)} %bitcast.99, f32[]{:T(128)} %bitcast.98, f32[]{:T(128)} %bitcast.95, ...), kind=kLoop, calls=%fused_computation.54 | loop fusion | flops 7864320 | bytes 18874400 | tf_op jit(solution)/shard_map/add | solution.py:50
  547.1 11.3 %fusion.23 = f32[1,1,1,8,1,256,256]{6,5,3,0,4,2,1:T(8,128)S(1)} fusion(f32[2,1,1,8,2,1,256,256]{7,6,4,3,0,5,2,1:T(8,128)} %bitcast.92, f32[2,1,1,8,2,1,256,256]{7,6,4,3,0,5,2,1:T(8,128)} %bitcast.97, f32[]{:T(128)} %bitcast.103, f32[]{:T(128)} %bitcast.102, f32[]{:T(128)} %bitcast.100, f32[]{:T(128)} %bitcast.99, f32[]{:T(128)} %bitcast.98, f32[]{:T(128)} %bitcast.95, ...), kind=kLoop, calls=%fused_computation.49 | loop fusion | flops 7864320 | bytes 18874400 | tf_op jit(solution)/shard_map/sub | solution.py:49
  559.0 0.9 pad_maximum_fusion.3
  559.8 0.9 copy.171
  560.7 4.9 copy.172
  565.6 101.3 %all_to_all.5 = f32[2,1,1,16,256,256]{5,3,0,2,1,4:T(8,128)S(1)} all-to-all(f32[2,1,1,16,256,256]{5,3,0,2,1,4:T(8,128)S(1)} %copy.172), channel_id=1, replica_groups=mesh['wide'=16,'narrow'=8] {'wide'}, dimensions={4} | all-to-all | bytes 16777216 | tf_op jit(solution)/shard_map/all_to_all | solution.py:62
  666.8 8.3 %copy.173 = f32[2,1,1,16,256,256]{5,4,3,2,1,0:T(8,128)} copy(f32[2,1,1,16,256,256]{5,3,0,2,1,4:T(8,128)S(1)} %all_to_all.5) | data formatting | bytes 16777216 | tf_op jit(solution)/shard_map/all_to_all | solution.py:62
  (38 shorter events, 6.2 us)
Async XLA Ops:
  0.0 5.5 copy-start.2
  5.5 4.5 copy-start.10
  10.0 3.5 copy-start.11
  38.2 7.5 %copy-start.1 = (f32[16,256,256]{2,1,0:T(8,128)}, f32[16,256,256]{2,1,0:T(8,128)S(1)}, u32[]{:S(2)}) copy-start(f32[16,256,256]{2,1,0:T(8,128)S(1)} %convolution_add_fusion) | copy-start | bytes 12582916
  45.7 4.5 copy-start
  50.2 22.7 %collective-permute-start = (f32[2,1,1,16,256,256]{4,5,3,2,1,0:T(8,128)}, f32[2,1,1,16,256,256]{4,5,3,2,1,0:T(8,128)}, u32[]{:S(2)}, u32[]{:S(2)}) collective-permute-start(f32[2,1,1,16,256,256]{4,5,3,2,1,0:T(8,128)} %pad_maximum_fusion), channel_id=1, source_target_pairs={{0,8},{8,0},{16,24},{24,16},{32,40},{40,32},{48,56},{56,48},{64,72... | collective-permute-start | bytes 25165832 | tf_op jit(solution)/shard_map/ppermute | solution.py:10
  68.6 2.9 copy-start.12
  91.4 12.4 %copy-start.7 = (f32[1,1,1,8,1,1,256,256]{7,6,3,5,4,2,1,0:T(8,128)S(1)}, f32[1,1,1,8,1,1,256,256]{7,6,3,5,4,2,1,0:T(8,128)}, u32[]{:S(2)}) copy-start(f32[1,1,1,8,1,1,256,256]{7,6,3,5,4,2,1,0:T(8,128)} %copy.187) | copy-start | bytes 6291460
  91.4 12.4 %copy-start.8 = (f32[1,1,1,8,1,1,256,256]{7,6,3,5,4,2,1,0:T(8,128)S(1)}, f32[1,1,1,8,1,1,256,256]{7,6,3,5,4,2,1,0:T(8,128)}, u32[]{:S(2)}) copy-start(f32[1,1,1,8,1,1,256,256]{7,6,3,5,4,2,1,0:T(8,128)} %copy.184) | copy-start | bytes 6291460
  91.4 12.4 %copy-start.9 = (f32[1,1,1,8,1,1,256,256]{7,6,3,5,4,2,1,0:T(8,128)S(1)}, f32[1,1,1,8,1,1,256,256]{7,6,3,5,4,2,1,0:T(8,128)}, u32[]{:S(2)}) copy-start(f32[1,1,1,8,1,1,256,256]{7,6,3,5,4,2,1,0:T(8,128)} %copy.183) | copy-start | bytes 6291460
  103.3 1.6 copy-start.3
  103.3 2.2 copy-start.4
  103.3 2.8 copy-start.5
  103.3 3.4 copy-start.6
  118.1 182.3 %collective-permute-start.1 = (f32[2,1,1,16,256,256]{5,4,3,0,2,1:T(8,128)}, f32[2,1,1,16,256,256]{5,4,3,0,2,1:T(8,128)S(1)}, u32[]{:S(2)}, u32[]{:S(2)}) collective-permute-start(f32[2,1,1,16,256,256]{5,4,3,0,2,1:T(8,128)} %bitcast.372), channel_id=1, source_target_pairs={{0,32},{8,40},{16,48},{24,56},{32,0},{40,8},{48,16},{56,24},{64,96... | collective-permute-start | bytes 25165832 | tf_op jit(solution)/shard_map/ppermute | solution.py:10
  329.9 183.1 %collective-permute-start.2 = (f32[2,1,1,16,256,256]{5,4,3,0,2,1:T(8,128)}, f32[2,1,1,16,256,256]{5,4,3,0,2,1:T(8,128)}, u32[]{:S(2)}, u32[]{:S(2)}) collective-permute-start(f32[2,1,1,16,256,256]{5,4,3,0,2,1:T(8,128)} %bitcast.96), channel_id=1, source_target_pairs={{0,2},{1,3},{2,0},{3,1},{4,6},{5,7},{6,4},{7,5},{8,10},{9,11},{10,... | collective-permute-start | bytes 25165832 | tf_op jit(solution)/shard_map/ppermute | solution.py:10
where the time goes:
time: 686 us; the launch traced here: 675 us
  waiting for transfers between devices  351 us (51%)
  other arithmetic  104 us (15%)
  blocking collectives  101 us (15%)
  local copies, waits for them, and re-layouts  66.9 us (10%)
  matrix products  45.6 us (7%)
    ppermute x3, waiting for transfers between devices, swapped(): lax.ppermute(x, axis, [(i, i ^ 1 << bit) for i in range(lax.axis_size(axi...  351 us
    all_to_all x1, blocking collectives, remap_qubits(): lax.all_to_all(state, 'wide', split_axis=4, concat_axis=4, tiled=True)  101 us
    sub x6, other arithmetic, partner_gate(): total_real + coef_real * amplitude[0] - coef_imag * amplitude[1]  53.5 us
    add x4, other arithmetic, partner_gate(): total_imag + coef_real * amplitude[1] + coef_imag * amplitude[0]  34.8 us
    unnamed x34, local copies, waits for them, and re-layouts  25.4 us
  transfers between devices with their start and end apart: 3, of which 2 were waited for; matrix products, arithmetic and copies ran while one was open for 5% of the time, Pallas kernels for 0%

commit v1 on v0

v1 whole, which is shorter than its diff:
```python
import functools

import jax
import jax.numpy as jnp
from jax import lax
from jax.experimental import pallas as pl
from jax.experimental.pallas import tpu as pltpu
from jax.sharding import PartitionSpec as P

f32, bf16 = jnp.float32, jnp.bfloat16
G = 256
ROWS = 16
CHUNK = 4


def hbm(x):
    return pltpu.with_memory_space_constraint(x, pltpu.HBM)


def split(x):
    high = x.astype(bf16)
    return high, (x - high.astype(f32)).astype(bf16)


def prep_kernel(g_ref, high_ref, low_ref):
    real, imag = g_ref[0], g_ref[1]
    for (row, col), part in (((0, 0), real), ((0, 1), -imag), ((1, 0), imag), ((1, 1), real)):
        high, low = split(part)
        high_ref[row * G : (row + 1) * G, col * G : (col + 1) * G] = high
        low_ref[row * G : (row + 1) * G, col * G : (col + 1) * G] = low


def prepare(gate):
    return pl.pallas_call(
        prep_kernel,
        out_shape=[jax.ShapeDtypeStruct((2 * G, 2 * G), bf16)] * 2,
        cost_estimate=pl.CostEstimate(flops=1, bytes_accessed=1, transcendentals=0),
        compiler_params=pltpu.CompilerParams(vmem_limit_bytes=60 << 20),
        name="prep",
    )(gate)


def merged_kernel(start_ref, x_ref, low_high, low_low, mid_high, mid_low, o_ref):
    x = jnp.concatenate([x_ref[0, 0], x_ref[1, 0]], axis=1)
    x_high, x_low = split(x)
    transposed = (((1,), (1,)), ((), ()))

    def right(a, b):
        return lax.dot_general(a, b, transposed, preferred_element_type=f32)

    def left(a, b):
        return jnp.dot(a, b, preferred_element_type=f32)

    t = right(x_high, low_high[...]) + right(x_high, low_low[...]) + right(x_low, low_high[...])
    t = jnp.concatenate([t[:, :G], t[:, G:]], axis=0)
    t_high, t_low = split(t)
    s = left(mid_high[...], t_high) + left(mid_high[...], t_low) + left(mid_low[...], t_high)
    o_ref[:, 0, 0] = s[:G].reshape(G // ROWS, ROWS, G)
    o_ref[:, 1, 0] = s[G:].reshape(G // ROWS, ROWS, G)


def merged(x, start, gates, count, weight=1):
    whole = pl.BlockSpec((2 * G, 2 * G), lambda i, s: (0, 0))
    return pl.pallas_call(
        merged_kernel,
        out_shape=jax.ShapeDtypeStruct((G // ROWS, 2, count, ROWS, G), f32),
        grid_spec=pltpu.PrefetchScalarGridSpec(
            num_scalar_prefetch=1,
            grid=(count,),
            in_specs=[pl.BlockSpec((2, 1, G, G), lambda i, s: (0, s[0] + i, 0, 0))] + [whole] * 4,
            out_specs=pl.BlockSpec((G // ROWS, 2, 1, ROWS, G), lambda i, s: (0, 0, i, 0, 0)),
        ),
        cost_estimate=pl.CostEstimate(
            flops=weight, bytes_accessed=1, transcendentals=0
        ),
        compiler_params=pltpu.CompilerParams(vmem_limit_bytes=60 << 20),
        name="merged",
    )(start, hbm(x), *gates)


def combine(coef, amps):
    outs = []
    for row in range(4):
        real = imag = None
        for col in range(4):
            cr, ci = coef(row, col)
            ar, ai = amps[col]
            real = cr * ar if real is None else real + cr * ar
            real = real - ci * ai
            imag = cr * ai if imag is None else imag + cr * ai
            imag = imag + ci * ar
        outs.append((real, imag))
    return outs


def pair_kernel(bit_ref, gate_ref, own_ref, far_ref, *refs):
    out_ref, back_ref, scratch = refs[-3:]
    own = bit_ref[0]
    sources = (own_ref, far_ref)
    targets = (out_ref, back_ref)

    def plain(k):
        def coef(row, col):
            return gate_ref[((2 * k) * 4 + row) * 4 + col], gate_ref[((2 * k + 1) * 4 + row) * 4 + col]

        return coef

    narrow_bit = (own, 1 - own)

    def narrow(row, col):
        r = 2 * narrow_bit[row >> 1] + (row & 1)
        c = 2 * narrow_bit[col >> 1] + (col & 1)
        at = 4 * r + c
        return gate_ref[64 + at], gate_ref[80 + at]

    def tile(step, carry):
        lanes = pl.ds(pl.multiple_of(step * 128, 128), 128)
        for n in range(2):
            for w0 in range(2):
                for h0 in range(2):
                    where = [(w2, w0, 2 * h1 + h0) for w2 in range(2) for h1 in range(2)]
                    amps = [tuple(sources[n][a, b, c, h, :, lanes] for c in range(2)) for a, b, h in where]
                    for (a, b, h), value in zip(where, combine(plain(1), amps)):
                        for c in range(2):
                            scratch[n, a, b, c, h] = value[c]
        for w2 in range(2):
            for h1 in range(2):
                state = {}
                for n in range(2):
                    where = [(w0, h0) for w0 in range(2) for h0 in range(2)]
                    amps = [tuple(scratch[n, w2, w0, c, 2 * h1 + h0] for c in range(2)) for w0, h0 in where]
                    for (w0, h0), value in zip(where, combine(plain(0), amps)):
                        state[n, w0, h0] = value
                for w0 in range(2):
                    where = [(n, h0) for n in range(2) for h0 in range(2)]
                    amps = [state[n, w0, h0] for n, h0 in where]
                    for (n, h0), value in zip(where, combine(narrow, amps)):
                        for c in range(2):
                            targets[n][c, 2 * h1 + h0, w2, w0, :, lanes] = value[c]
        return carry

    lax.fori_loop(0, 2, tile, 0)


def pair(bit, gates, own, far, chunk, base, count, held):
    shape = (2, 2, 2, 2, 2, CHUNK, ROWS, G)
    source = pl.BlockSpec((None, 2, None, 2, 2, CHUNK, 8, G), lambda i, j, r, s, g: (i, 0, j, 0, 0, 0, base + r, 0))
    full = (2, 4, CHUNK, 2, 2, 2, 2, ROWS, G)
    back = (2, CHUNK, 2, 2, 2, 2, 8 * count, G)
    out_spec = pl.BlockSpec(
        (2, None, CHUNK, None, 2, None, 2, 8, G),
        lambda i, j, r, s, g: (0, 2 * s[0] + chunk, 0, i, 0, j, 0, base + r, 0),
    )
    back_spec = pl.BlockSpec((2, CHUNK, None, 2, None, 2, 8, G), lambda i, j, r, s, g: (0, 0, i, 0, j, 0, r, 0))
    extra = [] if held is None else [held.reshape(full)]
    held, back = pl.pallas_call(
        pair_kernel,
        out_shape=[jax.ShapeDtypeStruct(full, f32), jax.ShapeDtypeStruct(back, f32)],
        grid_spec=pltpu.PrefetchScalarGridSpec(
            num_scalar_prefetch=2,
            grid=(2, 2, count),
            in_specs=[source, source] + [pl.BlockSpec(memory_space=pl.ANY)] * len(extra),
            out_specs=[out_spec, back_spec],
            scratch_shapes=[pltpu.VMEM((2, 2, 2, 2, CHUNK, 8, 128), f32)],
        ),
        input_output_aliases={4: 0} if extra else {},
        cost_estimate=pl.CostEstimate(flops=1, bytes_accessed=1, transcendentals=0),
        compiler_params=pltpu.CompilerParams(vmem_limit_bytes=16 << 20),
        name="pair",
    )(bit, gates, own.reshape(shape), far.reshape(shape), *extra)
    return held, back.reshape(2, CHUNK, 16, 8 * count, G)


def place_kernel(bit_ref, piece_ref, held_ref, out_ref):
    out_ref[...] = piece_ref[...]


def place(bit, piece, chunk, base, count, held, weight=1):
    full = (2, 4, CHUNK, 16, ROWS, G)
    return pl.pallas_call(
        place_kernel,
        out_shape=jax.ShapeDtypeStruct(full, f32),
        grid_spec=pltpu.PrefetchScalarGridSpec(
            num_scalar_prefetch=1,
            grid=(CHUNK,),
            in_specs=[
                pl.BlockSpec((2, 1, 16, 8 * count, G), lambda h, s: (0, h, 0, 0, 0)),
                pl.BlockSpec(memory_space=pl.ANY),
            ],
            out_specs=pl.BlockSpec(
                (2, None, 1, 16, 8 * count, G), lambda h, s: (0, 2 * (1 - s[0]) + chunk, h, 0, base, 0)
            ),
        ),
        input_output_aliases={2: 0},
        cost_estimate=pl.CostEstimate(flops=weight, bytes_accessed=1, transcendentals=0),
        compiler_params=pltpu.CompilerParams(vmem_limit_bytes=16 << 20),
        name="place",
    )(bit, piece, held.reshape(full))


def body(amplitudes, low_gate, mid_gate, pair_gates):
    x = amplitudes.reshape(2, 16, G, G)
    bit = lax.axis_index("narrow") >> 1 & 1
    bits = bit.reshape(1).astype(jnp.int32)
    partners = [(i, i ^ 2) for i in range(lax.axis_size("narrow"))]

    def swapped(value):
        return lax.ppermute(value, "narrow", partners)

    def remap(value):
        return lax.all_to_all(value, "wide", split_axis=0, concat_axis=0, tiled=True)

    barrier = lax.optimization_barrier

    def piece(bit, k):
        return lax.dynamic_slice_in_dim(x, 8 * (1 - bit) + CHUNK * k, CHUNK, 1)

    bits, low_gate, sent = barrier((bits, low_gate, piece(bit, 0)))
    arrived = [swapped(sent), swapped(piece(bits[0], 1))]
    gates = (*prepare(low_gate), *prepare(mid_gate))
    flat = pair_gates.reshape(96)
    zero = jnp.zeros((1,), jnp.int32)

    own0 = remap(merged(x, 8 * bits, gates, CHUNK))
    first = merged(arrived[0], zero, gates, CHUNK)
    bits1, first = barrier((bits, first))
    own1 = remap(merged(x, 8 * bits1 + CHUNK, gates, CHUNK))
    far0 = remap(first)
    pieces = {}
    held, pieces[0, 0] = pair(bits, flat, own0, far0, 0, 0, 2, None)
    last, pieces[0, 0] = barrier((arrived[1], pieces[0, 0]))
    far1 = remap(merged(last, zero, gates, CHUNK, 20000000000))
    for half in range(2):
        held, pieces[1, half] = pair(bits, flat, own1, far1, 1, half, 1, held)
    backs = {key: swapped(piece) for key, piece in pieces.items()}
    held = place(bits, backs[0, 0], 0, 0, 2, held, 20000000000)
    for half in range(2):
        held = place(bits, backs[1, half], 1, half, 1, held, 1000000000)
    return held.reshape(amplitudes.shape)


def solution(mesh):
    in_specs = (P(None, "wide", "narrow", None, None, None), P(), P(), P())
    out_specs = P(None, "wide", "narrow", None, None, None)
    return jax.shard_map(body, mesh=mesh, in_specs=in_specs, out_specs=out_specs, check_vma=False)
```

time: 686 us -> 223 us (0.33); the launches traced: 675 us -> 221 us
  waiting for transfers between devices: 351 us -> 87.3 us
  other arithmetic: 104 us -> 0 us
  blocking collectives: 101 us -> 32.4 us
  Pallas kernels: 0 us -> 62 us
  local copies, waits for them, and re-layouts: 66.9 us -> 9.18 us
  matrix products: 45.6 us -> 0 us
  starting transfers between devices: 5.71 us -> 30.5 us
    ppermute x3 -> x5, waiting for transfers between devices: 351 us -> 63.1 us  [swapped(): return lax.ppermute(value, 'narrow', partners)]
    all_to_all x1, blocking collectives: 101 us -> 32.4 us  [remap(): lax.all_to_all(value, 'wide', split_axis=0, concat_axis=0, tiled=True)]
    pallas_call x0 -> x12, Pallas kernels: none -> 62 us  [the longest x4 29 us: merged(): pl.pallas_call(merged_kernel, out_shape=jax.ShapeDtypeStruct((G // ROWS,...]
    sub x6 -> x0, other arithmetic: 53.5 us -> none  [partner_gate(): total_real + coef_real * amplitude[0] - coef_imag * amplitude[1]]
    dot_general x8 -> x0, matrix products: 45.6 us -> none  [the longest x1 7.46 us: apply_merged(): jnp.einsum('abhml,im->abhil', first_imag, mid_imag, precision=highest)]
    add x4 -> x0, other arithmetic: 34.8 us -> none  [partner_gate(): total_imag + coef_real * amplitude[1] + coef_imag * amplitude[0]]
    all_to_all x0 -> x3, waiting for transfers between devices: none -> 24.2 us  [remap(): lax.all_to_all(value, 'wide', split_axis=0, concat_axis=0, tiled=True)]
    slice x10 -> x0, local copies, waits for them, and re-layouts: 23.4 us -> none  [the longest x2 11.5 us: partner_gate(): amplitude[1]]
  transfers between devices with their start and end apart: 3 -> 8, of which waited for: 2 -> 5; matrix products, arithmetic and copies ran while one was open for 5% -> 1% of each run, Pallas kernels for 0% -> 27%
where the time goes in v1:
time: 223 us; the launch traced here: 221 us
  waiting for transfers between devices  87.3 us (39%)
  Pallas kernels  62 us (28%)
  blocking collectives  32.4 us (15%)
  starting transfers between devices  30.5 us (14%)
  local copies, waits for them, and re-layouts  9.18 us (4%)
    ppermute x5, waiting for transfers between devices, swapped(): return lax.ppermute(value, 'narrow', partners)  63.1 us
    all_to_all x1, blocking collectives, remap(): lax.all_to_all(value, 'wide', split_axis=0, concat_axis=0, tiled=True)  32.4 us
    pallas_call x4, Pallas kernels, merged(): pl.pallas_call(merged_kernel, out_shape=jax.ShapeDtypeStruct((G // ROWS,...  29 us
    all_to_all x3, waiting for transfers between devices, remap(): lax.all_to_all(value, 'wide', split_axis=0, concat_axis=0, tiled=True)  24.2 us
    pallas_call x3, Pallas kernels, pair(): pl.pallas_call(pair_kernel, out_shape=[jax.ShapeDtypeStruct(full, f32), j...  21.8 us
    all_to_all x3, starting transfers between devices, remap(): lax.all_to_all(value, 'wide', split_axis=0, concat_axis=0, tiled=True)  20.8 us
    ppermute x5, starting transfers between devices, swapped(): return lax.ppermute(value, 'narrow', partners)  9.74 us
    pallas_call x3, Pallas kernels, place(): pl.pallas_call(place_kernel, out_shape=jax.ShapeDtypeStruct(full, f32), g...  7 us
  transfers between devices with their start and end apart: 8, of which 5 were waited for; matrix products, arithmetic and copies ran while one was open for 1% of the time, Pallas kernels for 27%

profile of v1, /device:TPU:1, one launch (start us, length us, event | category | flops | bytes accessed | tf_op | source)
XLA Modules:
  0.0 221.5 jit_solution(6757440663482366186)
XLA Ops:
  0.0 3.1 %dynamic-slice_bitcast_fusion.1 = f32[2,4,256,256]{3,2,1,0:T(8,128)} fusion(f32[2,1,1,16,256,256]{5,4,3,2,1,0:T(8,128)} %param.4, s32[]{:T(128)S(6)} %select_n.6), kind=kLoop, calls=%fused_computation.1 | loop fusion | bytes 4194308 | tf_op jit(solution)/shard_map/dynamic_slice | solution.py:216
  3.1 3.7 %collective-permute-start = (f32[2,4,256,256]{3,2,1,0:T(8,128)}, f32[2,4,256,256]{3,2,1,0:T(8,128)}, u32[]{:S(2)}, u32[]{:S(2)}) collective-permute-start(f32[2,4,256,256]{3,2,1,0:T(8,128)} %dynamic-slice_bitcast_fusion.1), channel_id=1, source_target_pairs={{0,2},{1,3},{2,0},{3,1},{4,6},{5,7},{6,4},{7,5},{8,10},{9,11},{10,... | collective-permute-start | bytes 6291464 | tf_op jit(solution)/shard_map/ppermute | solution.py:208
  6.8 2.1 prep.3
  9.0 2.1 prep.2
  11.1 7.2 %merged.6 = f32[16,2,4,16,256]{4,3,2,1,0:T(8,128)} custom-call(s32[1]{0:T(128)S(6)} %mul.16.start_ref, f32[2,16,256,256]{3,2,1,0:T(8,128)} %bitcast.27, bf16[512,512]{1,0:T(8,128)(2,1)} %get-tuple-element.25.low_high, bf16[512,512]{1,0:T(8,128)(2,1)} %get-tuple-element.26.low_low, bf16[512,512]{1,0:T(8,128)(2,1)} %get-tuple-element.27.mid_high, ...), custom_call_target="tpu_custom_call" | custom-call | flops 1 | bytes 1 | tf_op jit(solution)/shard_map/merged/pallas_call | solution.py:64
  18.3 6.6 %all-to-all-start.1 = ((f32[16,2,4,16,256]{4,3,2,1,0:T(8,128)}), f32[16,2,4,16,256]{4,3,2,1,0:T(8,128)S(1)}, u32[]{:S(2)}, u32[]{:S(2)}) async-start(f32[16,2,4,16,256]{4,3,2,1,0:T(8,128)} %merged.6), calls=%async_computation.1 | async-start | bytes 4194304 | tf_op jit(solution)/shard_map/all_to_all | solution.py:211
  25.0 3.1 %dynamic-slice_bitcast_fusion = f32[2,4,256,256]{3,2,1,0:T(8,128)} fusion(f32[2,1,1,16,256,256]{5,4,3,2,1,0:T(8,128)} %param.4, s32[]{:T(128)S(6)} %select_n.7), kind=kLoop, calls=%fused_computation | loop fusion | bytes 4194308 | tf_op jit(solution)/shard_map/dynamic_slice | solution.py:216
  28.0 0.1 collective-permute-start.1
  28.1 24.1 %collective-permute-done.x_ref = f32[2,4,256,256]{3,2,1,0:T(8,128)} collective-permute-done((f32[2,4,256,256]{3,2,1,0:T(8,128)}, f32[2,4,256,256]{3,2,1,0:T(8,128)}, u32[]{:S(2)}, u32[]{:S(2)}) %collective-permute-start) | collective-permute-done | bytes 2097184 | tf_op jit(solution)/shard_map/ppermute | solution.py:208
  52.2 7.3 %merged.4 = f32[16,2,4,16,256]{4,3,2,1,0:T(8,128)} custom-call(s32[1]{0:T(128)} %constant.23.clone.1.start_ref, f32[2,4,256,256]{3,2,1,0:T(8,128)} %collective-permute-done.x_ref, bf16[512,512]{1,0:T(8,128)(2,1)} %get-tuple-element.25.low_high, bf16[512,512]{1,0:T(8,128)(2,1)} %get-tuple-element.26.low_low, bf16[512,512]{1,0:T(8,128)(2,1)} %get-tuple-element.27.mid_high, ...), custom_call_target="tpu_custom_call" | custom-call | flops 1 | bytes 1 | tf_op jit(solution)/shard_map/merged/pallas_call | solution.py:64
  59.5 0.0 all-to-all-done.1
  59.5 0.0 copy-start
  59.5 1.3 copy-done
  60.8 8.4 %all-to-all-start.2 = ((f32[16,2,4,16,256]{4,3,2,1,0:T(8,128)}), f32[16,2,4,16,256]{4,3,2,1,0:T(8,128)}, u32[]{:S(2)}, u32[]{:S(2)}) async-start(f32[16,2,4,16,256]{4,3,2,1,0:T(8,128)} %merged.4), calls=%async_computation.2 | async-start | bytes 4194304 | tf_op jit(solution)/shard_map/all_to_all | solution.py:211
  69.2 7.3 %merged.5 = f32[16,2,4,16,256]{4,3,2,1,0:T(8,128)} custom-call(s32[1]{0:T(128)S(6)} %add.21.start_ref, f32[2,16,256,256]{3,2,1,0:T(8,128)} %bitcast.28, bf16[512,512]{1,0:T(8,128)(2,1)} %get-tuple-element.25.low_high, bf16[512,512]{1,0:T(8,128)(2,1)} %get-tuple-element.26.low_low, bf16[512,512]{1,0:T(8,128)(2,1)} %get-tuple-element.27.mid_high, ...), custom_call_target="tpu_custom_call" | custom-call | flops 1 | bytes 1 | tf_op jit(solution)/shard_map/merged/pallas_call | solution.py:64
  76.5 0.0 copy-start.2
  76.5 19.8 %all-to-all-done.2 = f32[16,2,4,16,256]{4,3,2,1,0:T(8,128)} async-done(((f32[16,2,4,16,256]{4,3,2,1,0:T(8,128)}), f32[16,2,4,16,256]{4,3,2,1,0:T(8,128)}, u32[]{:S(2)}, u32[]{:S(2)}) %all-to-all-start.2) | async-done | bytes 2097184 | tf_op jit(solution)/shard_map/all_to_all | solution.py:211
  96.2 5.8 %all-to-all-start = ((f32[16,2,4,16,256]{4,3,2,1,0:T(8,128)}), f32[16,2,4,16,256]{4,3,2,1,0:T(8,128)S(1)}, u32[]{:S(2)}, u32[]{:S(2)}) async-start(f32[16,2,4,16,256]{4,3,2,1,0:T(8,128)} %merged.5), calls=%async_computation | async-start | bytes 4194304 | tf_op jit(solution)/shard_map/all_to_all | solution.py:211
  102.1 0.0 copy-done.2
  102.1 0.1 reshape.49.gate_ref
  102.2 0.0 copy-start.1
  102.2 1.6 copy-done.1
  103.8 10.7 %pair.3 = (f32[2,4,4,2,2,2,2,16,256]{8,7,6,5,4,3,2,1,0:T(8,128)}, f32[2,4,2,2,2,2,16,256]{7,6,5,4,3,2,1,0:T(8,128)}) custom-call(s32[1]{0:T(128)} %bitcast.bit_ref, f32[96]{0:T(128)S(1)} %reshape.49.gate_ref, f32[2,2,2,2,2,4,16,256]{7,6,5,4,3,2,1,0:T(8,128)S(1)} %bitcast.23, f32[2,2,2,2,2,4,16,256]{7,6,5,4,3,2,1,0:T(8,128)} %bitcast.8.far_ref), custom_call_target="tpu_custom_call" | custom-call | flops 1 | bytes 1 | tf_op jit(solution)/shard_map/pair/pallas_call | solution.py:156
  114.5 0.0 collective-permute-done.1.x_ref
  114.5 2.9 %collective-permute-start.4 = (f32[2,4,16,16,256]{4,3,2,1,0:T(8,128)}, f32[2,4,16,16,256]{4,3,2,1,0:T(8,128)}, u32[]{:S(2)}, u32[]{:S(2)}) collective-permute-start(f32[2,4,16,16,256]{4,3,2,1,0:T(8,128)} %bitcast.9), channel_id=1, source_target_pairs={{0,2},{1,3},{2,0},{3,1},{4,6},{5,7},{6,4},{7,5},{8,10},{9,11},{10,... | collective-permute-start | bytes 6291464 | tf_op jit(solution)/shard_map/ppermute | solution.py:208
  117.4 7.2 %merged.7 = f32[16,2,4,16,256]{4,3,2,1,0:T(8,128)} custom-call(s32[1]{0:T(128)} %constant.23.clone.1.start_ref, f32[2,4,256,256]{3,2,1,0:T(8,128)} %collective-permute-done.1.x_ref, bf16[512,512]{1,0:T(8,128)(2,1)} %get-tuple-element.25.low_high, bf16[512,512]{1,0:T(8,128)(2,1)} %get-tuple-element.26.low_low, bf16[512,512]{1,0:T(8,128)(2,1)} %get-tuple-element.27.mid_high, ...), custom_call_target="tpu_custom_call" | custom-call | flops 20000000000 | bytes 1 | tf_op jit(solution)/shard_map/merged/pallas_call | solution.py:64
  124.7 4.4 %all-to-all-done = f32[16,2,4,16,256]{4,3,2,1,0:T(8,128)S(1)} async-done(((f32[16,2,4,16,256]{4,3,2,1,0:T(8,128)}), f32[16,2,4,16,256]{4,3,2,1,0:T(8,128)S(1)}, u32[]{:S(2)}, u32[]{:S(2)}) %all-to-all-start) | async-done | bytes 2097184 | tf_op jit(solution)/shard_map/all_to_all | solution.py:211
  129.1 32.4 %all_to_all.20 = f32[16,2,4,16,256]{4,3,2,1,0:T(8,128)S(1)} all-to-all(f32[16,2,4,16,256]{4,3,2,1,0:T(8,128)} %merged.7), channel_id=1, replica_groups=mesh['wide'=16,'narrow'=8] {'wide'}, dimensions={0} | all-to-all | bytes 4194304 | tf_op jit(solution)/shard_map/all_to_all | solution.py:211
  161.5 5.5 %pair.4 = (f32[2,4,4,2,2,2,2,16,256]{8,7,6,5,4,3,2,1,0:T(8,128)}, f32[2,4,2,2,2,2,8,256]{7,6,5,4,3,2,1,0:T(8,128)S(1)}) custom-call(s32[1]{0:T(128)} %bitcast.bit_ref, f32[96]{0:T(128)S(1)} %reshape.49.gate_ref, f32[2,2,2,2,2,4,16,256]{7,6,5,4,3,2,1,0:T(8,128)S(1)} %bitcast.19, ...), custom_call_target="tpu_custom_call", output_to_operand_aliasing={{0}: (4, {})} | custom-call | flops 1 | bytes 1 | tf_op jit(solution)/shard_map/pair/pallas_call | solution.py:156
  167.0 5.5 %pair.5 = (f32[2,4,4,2,2,2,2,16,256]{8,7,6,5,4,3,2,1,0:T(8,128)}, f32[2,4,2,2,2,2,8,256]{7,6,5,4,3,2,1,0:T(8,128)S(1)}) custom-call(s32[1]{0:T(128)} %bitcast.bit_ref, f32[96]{0:T(128)S(1)} %reshape.49.gate_ref, f32[2,2,2,2,2,4,16,256]{7,6,5,4,3,2,1,0:T(8,128)S(1)} %bitcast.20, ...), custom_call_target="tpu_custom_call", output_to_operand_aliasing={{0}: (4, {})} | custom-call | flops 1 | bytes 1 | tf_op jit(solution)/shard_map/pair/pallas_call | solution.py:156
  172.5 2.8 %collective-permute-start.3 = (f32[2,4,16,8,256]{4,3,2,1,0:T(8,128)S(1)}, f32[2,4,16,8,256]{4,3,2,1,0:T(8,128)S(1)}, u32[]{:S(2)}, u32[]{:S(2)}) collective-permute-start(f32[2,4,16,8,256]{4,3,2,1,0:T(8,128)S(1)} %bitcast.25), channel_id=1, source_target_pairs={{0,2},{1,3},{2,0},{3,1},{4,6},{5,7},{6,4},{7,5},{8,10},{9,11},{10,... | collective-permute-start | bytes 3145736 | tf_op jit(solution)/shard_map/ppermute | solution.py:208
  175.3 0.1 collective-permute-start.2
  175.5 0.0 collective-permute-done.4.piece_ref
  175.5 3.8 %place.3.held_ref = f32[2,4,4,16,16,256]{5,4,3,2,1,0:T(8,128)} custom-call(s32[1]{0:T(128)} %bitcast.bit_ref, f32[2,4,16,16,256]{4,3,2,1,0:T(8,128)} %collective-permute-done.4.piece_ref, f32[2,4,4,16,16,256]{5,4,3,2,1,0:T(8,128)} %bitcast.26), custom_call_target="tpu_custom_call", output_to_operand_aliasing={{}: (2, {})} | custom-call | flops 20000000000 | bytes 1 | tf_op jit(solution)/shard_map/place/pallas_call | solution.py:180
  179.3 18.2 %collective-permute-done.3.piece_ref = f32[2,4,16,8,256]{4,3,2,1,0:T(8,128)S(1)} collective-permute-done((f32[2,4,16,8,256]{4,3,2,1,0:T(8,128)S(1)}, f32[2,4,16,8,256]{4,3,2,1,0:T(8,128)S(1)}, u32[]{:S(2)}, u32[]{:S(2)}) %collective-permute-start.3) | collective-permute-done | bytes 1048608 | tf_op jit(solution)/shard_map/ppermute | solution.py:208
  197.4 1.6 place.4.held_ref
  199.0 20.9 %collective-permute-done.2.piece_ref = f32[2,4,16,8,256]{4,3,2,1,0:T(8,128)S(1)} collective-permute-done((f32[2,4,16,8,256]{4,3,2,1,0:T(8,128)S(1)}, f32[2,4,16,8,256]{4,3,2,1,0:T(8,128)S(1)}, u32[]{:S(2)}, u32[]{:S(2)}) %collective-permute-start.2) | collective-permute-done | bytes 1048608 | tf_op jit(solution)/shard_map/ppermute | solution.py:208
  219.9 1.6 place.5
Async XLA Ops:
  3.1 49.1 %collective-permute-start = (f32[2,4,256,256]{3,2,1,0:T(8,128)}, f32[2,4,256,256]{3,2,1,0:T(8,128)}, u32[]{:S(2)}, u32[]{:S(2)}) collective-permute-start(f32[2,4,256,256]{3,2,1,0:T(8,128)} %dynamic-slice_bitcast_fusion.1), channel_id=1, source_target_pairs={{0,2},{1,3},{2,0},{3,1},{4,6},{5,7},{6,4},{7,5},{8,10},{9,11},{10,... | collective-permute-start | bytes 6291464 | tf_op jit(solution)/shard_map/ppermute | solution.py:208
  18.3 41.2 %all-to-all-start.1 = ((f32[16,2,4,16,256]{4,3,2,1,0:T(8,128)}), f32[16,2,4,16,256]{4,3,2,1,0:T(8,128)S(1)}, u32[]{:S(2)}, u32[]{:S(2)}) async-start(f32[16,2,4,16,256]{4,3,2,1,0:T(8,128)} %merged.6), calls=%async_computation.1 | async-start | bytes 4194304 | tf_op jit(solution)/shard_map/all_to_all | solution.py:211
  28.0 86.5 %collective-permute-start.1 = (f32[2,4,256,256]{3,2,1,0:T(8,128)}, f32[2,4,256,256]{3,2,1,0:T(8,128)}, u32[]{:S(2)}, u32[]{:S(2)}) collective-permute-start(f32[2,4,256,256]{3,2,1,0:T(8,128)} %dynamic-slice_bitcast_fusion), channel_id=1, source_target_pairs={{0,2},{1,3},{2,0},{3,1},{4,6},{5,7},{6,4},{7,5},{8,10},{9,11},{10,... | collective-permute-start | bytes 6291464 | tf_op jit(solution)/shard_map/ppermute | solution.py:208
  59.5 1.3 copy-start
  60.8 35.4 %all-to-all-start.2 = ((f32[16,2,4,16,256]{4,3,2,1,0:T(8,128)}), f32[16,2,4,16,256]{4,3,2,1,0:T(8,128)}, u32[]{:S(2)}, u32[]{:S(2)}) async-start(f32[16,2,4,16,256]{4,3,2,1,0:T(8,128)} %merged.4), calls=%async_computation.2 | async-start | bytes 4194304 | tf_op jit(solution)/shard_map/all_to_all | solution.py:211
  76.5 25.6 %copy-start.2 = (f32[3,2,4,4]{3,2,1,0:T(4,128)S(1)}, f32[3,2,4,4]{3,2,1,0:T(4,128)}, u32[]{:S(2)}) copy-start(f32[3,2,4,4]{3,2,1,0:T(4,128)} %param.7) | copy-start | bytes 1156
  96.2 32.9 %all-to-all-start = ((f32[16,2,4,16,256]{4,3,2,1,0:T(8,128)}), f32[16,2,4,16,256]{4,3,2,1,0:T(8,128)S(1)}, u32[]{:S(2)}, u32[]{:S(2)}) async-start(f32[16,2,4,16,256]{4,3,2,1,0:T(8,128)} %merged.5), calls=%async_computation | async-start | bytes 4194304 | tf_op jit(solution)/shard_map/all_to_all | solution.py:211
  102.2 1.6 copy-start.1
  114.5 61.0 %collective-permute-start.4 = (f32[2,4,16,16,256]{4,3,2,1,0:T(8,128)}, f32[2,4,16,16,256]{4,3,2,1,0:T(8,128)}, u32[]{:S(2)}, u32[]{:S(2)}) collective-permute-start(f32[2,4,16,16,256]{4,3,2,1,0:T(8,128)} %bitcast.9), channel_id=1, source_target_pairs={{0,2},{1,3},{2,0},{3,1},{4,6},{5,7},{6,4},{7,5},{8,10},{9,11},{10,... | collective-permute-start | bytes 6291464 | tf_op jit(solution)/shard_map/ppermute | solution.py:208
  172.5 24.9 %collective-permute-start.3 = (f32[2,4,16,8,256]{4,3,2,1,0:T(8,128)S(1)}, f32[2,4,16,8,256]{4,3,2,1,0:T(8,128)S(1)}, u32[]{:S(2)}, u32[]{:S(2)}) collective-permute-start(f32[2,4,16,8,256]{4,3,2,1,0:T(8,128)S(1)} %bitcast.25), channel_id=1, source_target_pairs={{0,2},{1,3},{2,0},{3,1},{4,6},{5,7},{6,4},{7,5},{8,10},{9,11},{10,... | collective-permute-start | bytes 3145736 | tf_op jit(solution)/shard_map/ppermute | solution.py:208
  175.3 44.5 %collective-permute-start.2 = (f32[2,4,16,8,256]{4,3,2,1,0:T(8,128)S(1)}, f32[2,4,16,8,256]{4,3,2,1,0:T(8,128)S(1)}, u32[]{:S(2)}, u32[]{:S(2)}) collective-permute-start(f32[2,4,16,8,256]{4,3,2,1,0:T(8,128)S(1)} %bitcast.24), channel_id=1, source_target_pairs={{0,2},{1,3},{2,0},{3,1},{4,6},{5,7},{6,4},{7,5},{8,10},{9,11},{10,... | collective-permute-start | bytes 3145736 | tf_op jit(solution)/shard_map/ppermute | solution.py:208

commit v2 on v0

v2 whole, which is shorter than its diff:
```python
import jax
import jax.numpy as jnp
from jax import lax
from jax.experimental import pallas as pl
from jax.experimental.pallas import tpu as pltpu
from jax.sharding import PartitionSpec as P

f32, bf16 = jnp.float32, jnp.bfloat16
G = 256
ROWS = 16
CHUNK = 4
PAIR = 2


def cost(weight):
    return pl.CostEstimate(flops=weight, bytes_accessed=1, transcendentals=0)


def params(mib):
    return pltpu.CompilerParams(vmem_limit_bytes=mib << 20)


def hbm(x):
    return pltpu.with_memory_space_constraint(x, pltpu.HBM)


def split(x):
    high = x.astype(bf16)
    return high, (x - high.astype(f32)).astype(bf16)


def prep_kernel(low_ref, mid_ref, o_ref):
    for at, ref in enumerate((low_ref, mid_ref)):
        real, imag = ref[0], ref[1]
        for j, part in enumerate((real, imag - real, real + imag)):
            o_ref[at, j, 0], o_ref[at, j, 1] = split(part)


def prepare(low_gate, mid_gate):
    return pl.pallas_call(
        prep_kernel,
        out_shape=jax.ShapeDtypeStruct((2, 3, 2, G, G), bf16),
        cost_estimate=cost(1),
        compiler_params=params(60),
        name="prep",
    )(low_gate, mid_gate)


def merged_kernel(x_ref, g_ref, refs):

    def right(value, j):
        high, low = split(value)
        out = None
        for a, b in ((high, 0), (high, 1), (low, 0)):
            term = lax.dot_general(a, g_ref[0, j, b], (((1,), (1,)), ((), ())), preferred_element_type=f32)
            out = term if out is None else out + term
        return out

    def left(value, j):
        high, low = split(value)
        out = None
        for a, b in ((0, high), (0, low), (1, high)):
            term = jnp.dot(g_ref[1, j, a], b, preferred_element_type=f32)
            out = term if out is None else out + term
        return out

    def both(apply, real, imag):
        shared = apply(real + imag, 0)
        cross = apply(real, 1)
        return shared - apply(imag, 2), shared + cross

    firsts = [both(right, x_ref[0, i], x_ref[1, i]) for i in range(PAIR)]
    for i, first in enumerate(firsts):
        for c, value in enumerate(both(left, *first)):
            value = value.reshape(G // ROWS, ROWS, G)
            for at, o_ref in enumerate(refs):
                rows = ROWS // len(refs)
                o_ref[:, c, i] = value[:, at * rows : (at + 1) * rows]


def merged(x, start, gates, parts=1, part=0, held=(), weight=1):
    steps = CHUNK // PAIR
    rows = ROWS // parts
    out = jax.ShapeDtypeStruct((G // ROWS, 2, parts * CHUNK, rows, G), f32)
    spec = pl.BlockSpec((G // ROWS, 2, PAIR, rows, G), lambda i, s: (0, 0, part * steps + i, 0, 0))

    def kernel(start_ref, x_ref, g_ref, *refs):
        merged_kernel(x_ref, g_ref, refs[len(held) :])

    return pl.pallas_call(
        kernel,
        out_shape=[out] * parts,
        grid_spec=pltpu.PrefetchScalarGridSpec(
            num_scalar_prefetch=1,
            grid=(steps,),
            in_specs=[
                pl.BlockSpec((2, PAIR, G, G), lambda i, s: (0, s[0] * steps + i, 0, 0)),
                pl.BlockSpec((2, 3, 2, G, G), lambda i, s: (0, 0, 0, 0, 0)),
            ]
            + [pl.BlockSpec(memory_space=pl.ANY)] * len(held),
            out_specs=[spec] * parts,
        ),
        input_output_aliases={3 + j: j for j in range(len(held))},
        cost_estimate=cost(weight),
        compiler_params=params(60),
        name="merged",
    )(start, hbm(x), gates, *held)


def combine(coef, amps, rows=4):
    outs = []
    for row in range(rows):
        real = imag = None
        for col, (ar, ai) in enumerate(amps):
            cr, ci = coef(row, col)
            real = cr * ar - ci * ai if real is None else real + (cr * ar - ci * ai)
            imag = cr * ai + ci * ar if imag is None else imag + (cr * ai + ci * ar)
        outs.append((real, imag))
    return outs


def plain(gate_ref, k):
    def coef(row, col):
        return gate_ref[32 * k + 4 * row + col], gate_ref[32 * k + 16 + 4 * row + col]

    return coef


def narrow_coef(gate_ref, own):
    bit = (own, 1 - own)

    def coef(row, col):
        at = 64 + 4 * (2 * bit[row >> 1] + (row & 1)) + 2 * bit[col >> 1] + (col & 1)
        return gate_ref[at], gate_ref[at + 16]

    return coef


def wide_high(gate_ref, ref, out):
    for w0 in range(2):
        for h0 in range(2):
            where = [(w2, w0, 2 * h1 + h0) for w2 in range(2) for h1 in range(2)]
            amps = [(ref[a, b, 0, h], ref[a, b, 1, h]) for a, b, h in where]
            for (a, b, h), (real, imag) in zip(where, combine(plain(gate_ref, 1), amps)):
                out[a, b, 0, h], out[a, b, 1, h] = real, imag


def wide_low(gate_ref, ref, w2, h1):
    where = [(w0, h0) for w0 in range(2) for h0 in range(2)]
    amps = [(ref[w2, w0, 0, 2 * h1 + h0], ref[w2, w0, 1, 2 * h1 + h0]) for w0, h0 in where]
    return dict(zip(where, combine(plain(gate_ref, 0), amps)))


def local_kernel(gate_ref, x_ref, o_ref, scratch):
    wide_high(gate_ref, x_ref, scratch)
    for w2 in range(2):
        for h1 in range(2):
            for (w0, h0), (real, imag) in wide_low(gate_ref, scratch, w2, h1).items():
                o_ref[0, 2 * h1 + h0, w2, w0] = real
                o_ref[1, 2 * h1 + h0, w2, w0] = imag


def local(gates, x):
    return pl.pallas_call(
        local_kernel,
        out_shape=jax.ShapeDtypeStruct((2, CHUNK, 2, 2, 2, 2, ROWS, G), f32),
        grid_spec=pltpu.PrefetchScalarGridSpec(
            num_scalar_prefetch=1,
            grid=(2, 2, 2),
            in_specs=[pl.BlockSpec((None, 2, None, 2, 2, CHUNK, 8, G), lambda i, j, r, g: (i, 0, j, 0, 0, 0, r, 0))],
            out_specs=pl.BlockSpec((2, CHUNK, None, 2, None, 2, 8, G), lambda i, j, r, g: (0, 0, i, 0, j, 0, r, 0)),
            scratch_shapes=[pltpu.VMEM((2, 2, 2, CHUNK, 8, G), f32)],
        ),
        cost_estimate=cost(1),
        compiler_params=params(16),
        name="local",
    )(gates, x.reshape(2, 2, 2, 2, 2, CHUNK, ROWS, G)).reshape(2, CHUNK, G, G)


def narrow_kernel(bit_ref, gate_ref, own_ref, far_ref, *refs):
    out_ref = refs[-1]
    coef = narrow_coef(gate_ref, bit_ref[0])

    def tile(step, carry):
        rows = pl.ds(pl.multiple_of(step * 8, 8), 8)
        for h1 in range(2):
            amps = [
                tuple(ref[c, 2 * h1 + h0, rows, :] for c in range(2)) for ref in (own_ref, far_ref) for h0 in range(2)
            ]
            for h0, (real, imag) in enumerate(combine(coef, amps, 2)):
                out_ref[0, 2 * h1 + h0, rows, :] = real
                out_ref[1, 2 * h1 + h0, rows, :] = imag
        return carry

    lax.fori_loop(0, 8, tile, 0)


def narrow(bit, gates, own, far, group, held, weight=1):
    source = pl.BlockSpec((2, CHUNK, 64, G), lambda i, s, g: (0, 0, i, 0))
    extra = [] if held is None else [held.reshape(2, 4, CHUNK, G, G)]
    return pl.pallas_call(
        narrow_kernel,
        out_shape=jax.ShapeDtypeStruct((2, 4, CHUNK, G, G), f32),
        grid_spec=pltpu.PrefetchScalarGridSpec(
            num_scalar_prefetch=2,
            grid=(4,),
            in_specs=[source, source] + [pl.BlockSpec(memory_space=pl.ANY)] * len(extra),
            out_specs=pl.BlockSpec((2, None, CHUNK, 64, G), lambda i, s, g: (0, group, 0, i, 0)),
        ),
        input_output_aliases={4: 0} if extra else {},
        cost_estimate=cost(weight),
        compiler_params=params(16),
        name="narrow",
    )(bit, gates, own, far, *extra)


def pair_kernel(bit_ref, gate_ref, own_ref, far_ref, held_ref, out_ref, back_ref, scratch):
    for n, ref in enumerate((own_ref, far_ref)):
        wide_high(gate_ref, ref, scratch.at[n])
    coef = narrow_coef(gate_ref, bit_ref[0])
    for w2 in range(2):
        for h1 in range(2):
            state = [wide_low(gate_ref, scratch.at[n], w2, h1) for n in range(2)]
            for w0 in range(2):
                where = [(n, h0) for n in range(2) for h0 in range(2)]
                values = combine(coef, [state[n][w0, h0] for n, h0 in where])
                for (n, h0), (real, imag) in zip(where, values):
                    target = (out_ref, back_ref)[n]
                    target[0, 2 * h1 + h0, w2, w0] = real
                    target[1, 2 * h1 + h0, w2, w0] = imag


def pair(bit, gates, both, half, held):
    def source(part):
        return pl.BlockSpec(
            (None, 2, None, 2, 2, None, CHUNK, 8, G), lambda i, j, s, g: (i, 0, j, 0, 0, part, 0, 0, 0)
        )

    both = both.reshape(2, 2, 2, 2, 2, 2, CHUNK, 8, G)
    full = (2, 4, CHUNK, 2, 2, 2, 2, ROWS, G)
    back = (2, CHUNK, 2, 2, 2, 2, 8, G)
    held, back = pl.pallas_call(
        pair_kernel,
        out_shape=[jax.ShapeDtypeStruct(full, f32), jax.ShapeDtypeStruct(back, f32)],
        grid_spec=pltpu.PrefetchScalarGridSpec(
            num_scalar_prefetch=2,
            grid=(2, 2),
            in_specs=[source(0), source(1), pl.BlockSpec(memory_space=pl.ANY)],
            out_specs=[
                pl.BlockSpec(
                    (2, None, CHUNK, None, 2, None, 2, 8, G),
                    lambda i, j, s, g: (0, 2 * s[0], 0, i, 0, j, 0, half, 0),
                ),
                pl.BlockSpec((2, CHUNK, None, 2, None, 2, 8, G), lambda i, j, s, g: (0, 0, i, 0, j, 0, 0, 0)),
            ],
            scratch_shapes=[pltpu.VMEM((2, 2, 2, 2, CHUNK, 8, G), f32)],
        ),
        input_output_aliases={4: 0},
        cost_estimate=cost(1),
        compiler_params=params(16),
        name="pair",
    )(bit, gates, both, both, held.reshape(full))
    return held, back.reshape(2, CHUNK, G // ROWS, 8, G)


def place_kernel(bit_ref, piece_ref, held_ref, out_ref):
    out_ref[...] = piece_ref[...]


def place(bit, piece, half, held, weight=1):
    full = (2, 4, CHUNK, G // ROWS, ROWS, G)
    return pl.pallas_call(
        place_kernel,
        out_shape=jax.ShapeDtypeStruct(full, f32),
        grid_spec=pltpu.PrefetchScalarGridSpec(
            num_scalar_prefetch=1,
            grid=(CHUNK,),
            in_specs=[
                pl.BlockSpec((2, 1, G // ROWS, 8, G), lambda h, s: (0, h, 0, 0, 0)),
                pl.BlockSpec(memory_space=pl.ANY),
            ],
            out_specs=pl.BlockSpec(
                (2, None, 1, G // ROWS, 8, G), lambda h, s: (0, 2 * (1 - s[0]), h, 0, half, 0)
            ),
        ),
        input_output_aliases={2: 0},
        cost_estimate=cost(weight),
        compiler_params=params(16),
        name="place",
    )(bit, piece, held.reshape(full))


def body(amplitudes, low_gate, mid_gate, pair_gates):
    x = amplitudes.reshape(2, 16, G, G)
    bit = lax.axis_index("narrow") >> 1 & 1
    bits = bit.reshape(1).astype(jnp.int32)
    partners = [(i, i ^ 2) for i in range(lax.axis_size("narrow"))]
    barrier = lax.optimization_barrier

    def swapped(value):
        return lax.ppermute(value, "narrow", partners)

    def remap(value):
        return lax.all_to_all(value, "wide", split_axis=0, concat_axis=0, tiled=True)

    def group(value):
        return jnp.full((1,), value, jnp.int32)

    sent = lax.dynamic_slice_in_dim(x, 8 * (1 - bit), CHUNK, 1)
    bits, low_gate, sent = barrier((bits, low_gate, sent))
    arrived = swapped(sent)
    gates = prepare(low_gate, mid_gate)
    flat = pair_gates.reshape(96)

    first = local(flat, remap(merged(x, group(1), gates)[0]))
    own = merged(x, 2 * bits, gates, 2, 0)
    gates, own = barrier((gates, own))
    second = merged(x, group(3), gates)[0]
    second, first = barrier((second, first))
    second = local(flat, remap(second))
    far = merged(arrived, group(0), gates, 2, 1, own, 30000000000)
    held = narrow(bits, flat, first, swapped(first), 1, None, 50000000000)
    backs = []
    for half in range(2):
        held, back = pair(bits, flat, remap(far[half]), half, held)
        backs.append(swapped(back))
    held = narrow(bits, flat, second, swapped(second), 3, held, 10000000000)
    for half in range(2):
        held = place(bits, backs[half], half, held, 1000000000)
    return held.reshape(amplitudes.shape)


def solution(mesh):
    in_specs = (P(None, "wide", "narrow", None, None, None), P(), P(), P())
    out_specs = P(None, "wide", "narrow", None, None, None)
    return jax.shard_map(body, mesh=mesh, in_specs=in_specs, out_specs=out_specs, check_vma=False)
```

time: 686 us -> 197 us (0.29); the launches traced: 675 us -> 196 us
  waiting for transfers between devices: 351 us -> 92.6 us
  other arithmetic: 104 us -> 0 us
  blocking collectives: 101 us -> 0 us
  local copies, waits for them, and re-layouts: 66.9 us -> 6.05 us
  Pallas kernels: 0 us -> 60.6 us
  matrix products: 45.6 us -> 0 us
  starting transfers between devices: 5.71 us -> 36.7 us
    ppermute x3 -> x5, waiting for transfers between devices: 351 us -> 24.6 us  [swapped(): return lax.ppermute(value, 'narrow', partners)]
    all_to_all x1 -> x0, blocking collectives: 101 us -> none  [remap_qubits(): lax.all_to_all(state, 'wide', split_axis=4, concat_axis=4, tiled=True)]
    all_to_all x0 -> x4, waiting for transfers between devices: none -> 68.1 us  [remap(): lax.all_to_all(value, 'wide', split_axis=0, concat_axis=0, tiled=True)]
    pallas_call x0 -> x13, Pallas kernels: none -> 60.6 us  [the longest x4 22.7 us: merged(): pl.pallas_call(kernel, out_shape=[out] * parts, grid_spec=pltpu.PrefetchS...]
    sub x6 -> x0, other arithmetic: 53.5 us -> none  [partner_gate(): total_real + coef_real * amplitude[0] - coef_imag * amplitude[1]]
    dot_general x8 -> x0, matrix products: 45.6 us -> none  [the longest x1 7.46 us: apply_merged(): jnp.einsum('abhml,im->abhil', first_imag, mid_imag, precision=highest)]
    add x4 -> x0, other arithmetic: 34.8 us -> none  [partner_gate(): total_imag + coef_real * amplitude[1] + coef_imag * amplitude[0]]
    all_to_all x0 -> x4, starting transfers between devices: none -> 24.2 us  [remap(): lax.all_to_all(value, 'wide', split_axis=0, concat_axis=0, tiled=True)]
  transfers between devices with their start and end apart: 3 -> 9, of which waited for: 2 -> 6; matrix products, arithmetic and copies ran while one was open for 5% -> 0% of each run, Pallas kernels for 0% -> 30%
where the time goes in v2:
time: 197 us; the launch traced here: 196 us
  waiting for transfers between devices  92.6 us (47%)
  Pallas kernels  60.6 us (31%)
  starting transfers between devices  36.7 us (19%)
  local copies, waits for them, and re-layouts  6.05 us (3%)
    all_to_all x4, waiting for transfers between devices, remap(): lax.all_to_all(value, 'wide', split_axis=0, concat_axis=0, tiled=True)  68.1 us
    ppermute x5, waiting for transfers between devices, swapped(): return lax.ppermute(value, 'narrow', partners)  24.6 us
    all_to_all x4, starting transfers between devices, remap(): lax.all_to_all(value, 'wide', split_axis=0, concat_axis=0, tiled=True)  24.2 us
    pallas_call x4, Pallas kernels, merged(): pl.pallas_call(kernel, out_shape=[out] * parts, grid_spec=pltpu.PrefetchS...  22.7 us
    ppermute x5, starting transfers between devices, swapped(): return lax.ppermute(value, 'narrow', partners)  12.5 us
    pallas_call x2, Pallas kernels, pair(): pl.pallas_call(pair_kernel, out_shape=[jax.ShapeDtypeStruct(full, f32), j...  11.2 us
    pallas_call x2, Pallas kernels, narrow(): pl.pallas_call(narrow_kernel, out_shape=jax.ShapeDtypeStruct((2, 4, CHUNK...  10.8 us
    pallas_call x2, Pallas kernels, local(): pl.pallas_call(local_kernel, out_shape=jax.ShapeDtypeStruct((2, CHUNK, 2,...  10.1 us
  transfers between devices with their start and end apart: 9, of which 6 were waited for; matrix products, arithmetic and copies ran while one was open for 0% of the time, Pallas kernels for 30%

profile of v2, /device:TPU:1, one launch (start us, length us, event | category | flops | bytes accessed | tf_op | source)
XLA Modules:
  0.0 196.0 jit_solution(13945600734855879963)
XLA Ops:
  0.0 3.0 %dynamic-slice_bitcast_fusion = f32[2,4,256,256]{3,2,1,0:T(8,128)} fusion(f32[2,1,1,16,256,256]{5,4,3,2,1,0:T(8,128)} %param.4, s32[]{:T(128)S(6)} %select_n.3), kind=kLoop, calls=%fused_computation | loop fusion | bytes 4194308 | tf_op jit(solution)/shard_map/dynamic_slice | solution.py:309
  3.0 3.7 %collective-permute-start = (f32[2,4,256,256]{3,2,1,0:T(8,128)}, f32[2,4,256,256]{3,2,1,0:T(8,128)}, u32[]{:S(2)}, u32[]{:S(2)}) collective-permute-start(f32[2,4,256,256]{3,2,1,0:T(8,128)} %dynamic-slice_bitcast_fusion), channel_id=1, source_target_pairs={{0,2},{1,3},{2,0},{3,1},{4,6},{5,7},{6,4},{7,5},{8,10},{9,11},{10,... | collective-permute-start | bytes 6291464 | tf_op jit(solution)/shard_map/ppermute | solution.py:301
  6.8 2.7 %prep.1.g_ref = bf16[2,3,2,256,256]{4,3,2,1,0:T(8,128)(2,1)} custom-call(f32[2,256,256]{2,1,0:T(8,128)} %low_ref, f32[2,256,256]{2,1,0:T(8,128)} %mid_ref.1), custom_call_target="tpu_custom_call" | custom-call | flops 1 | bytes 1 | tf_op jit(solution)/shard_map/prep/pallas_call | solution.py:40
  9.5 5.6 %merged.7 = f32[16,2,4,16,256]{4,3,2,1,0:T(8,128)} custom-call(s32[1]{0:T(128)} %constant.20.clone.1.start_ref, f32[2,16,256,256]{3,2,1,0:T(8,128)} %bitcast.27, bf16[2,3,2,256,256]{4,3,2,1,0:T(8,128)(2,1)} %prep.1.g_ref), custom_call_target="tpu_custom_call" | custom-call | flops 1 | bytes 1 | tf_op jit(solution)/shard_map/merged/pallas_call | solution.py:90
  15.1 6.6 %all-to-all-start.2 = ((f32[16,2,4,16,256]{4,3,2,1,0:T(8,128)}), f32[16,2,4,16,256]{4,3,2,1,0:T(8,128)S(1)}, u32[]{:S(2)}, u32[]{:S(2)}) async-start(f32[16,2,4,16,256]{4,3,2,1,0:T(8,128)} %merged.7), calls=%async_computation.2 | async-start | bytes 4194304 | tf_op jit(solution)/shard_map/all_to_all | solution.py:304
  21.7 5.7 %merged.4 = (f32[16,2,8,8,256]{4,3,2,1,0:T(8,128)}, f32[16,2,8,8,256]{4,3,2,1,0:T(8,128)}) custom-call(s32[1]{0:T(128)S(6)} %mul.3.start_ref, f32[2,16,256,256]{3,2,1,0:T(8,128)} %bitcast.28, bf16[2,3,2,256,256]{4,3,2,1,0:T(8,128)(2,1)} %prep.1.g_ref), custom_call_target="tpu_custom_call" | custom-call | flops 1 | bytes 1 | tf_op jit(solution)/shard_map/merged/pallas_call | solution.py:90
  27.4 0.0 copy-start.2
  27.4 5.6 %merged.6 = f32[16,2,4,16,256]{4,3,2,1,0:T(8,128)} custom-call(s32[1]{0:T(128)} %constant.8.clone.1.start_ref, f32[2,16,256,256]{3,2,1,0:T(8,128)} %bitcast.29, bf16[2,3,2,256,256]{4,3,2,1,0:T(8,128)(2,1)} %prep.1.g_ref), custom_call_target="tpu_custom_call" | custom-call | flops 1 | bytes 1 | tf_op jit(solution)/shard_map/merged/pallas_call | solution.py:90
  33.0 0.0 copy-done.2
  33.0 0.1 reshape.47.gate_ref
  33.1 15.6 %all-to-all-done.2 = f32[16,2,4,16,256]{4,3,2,1,0:T(8,128)S(1)} async-done(((f32[16,2,4,16,256]{4,3,2,1,0:T(8,128)}), f32[16,2,4,16,256]{4,3,2,1,0:T(8,128)S(1)}, u32[]{:S(2)}, u32[]{:S(2)}) %all-to-all-start.2) | async-done | bytes 2097184 | tf_op jit(solution)/shard_map/all_to_all | solution.py:304
  48.8 5.1 %local.2 = f32[2,4,2,2,2,2,16,256]{7,6,5,4,3,2,1,0:T(8,128)} custom-call(f32[96]{0:T(128)S(1)} %reshape.47.gate_ref, f32[2,2,2,2,2,4,16,256]{7,6,5,4,3,2,1,0:T(8,128)S(1)} %bitcast.21), custom_call_target="tpu_custom_call" | custom-call | flops 1 | bytes 1 | tf_op jit(solution)/shard_map/local/pallas_call | solution.py:164
  53.8 0.0 collective-permute-start.1
  53.8 5.9 %all-to-all-start.3 = ((f32[16,2,4,16,256]{4,3,2,1,0:T(8,128)}), f32[16,2,4,16,256]{4,3,2,1,0:T(8,128)S(1)}, u32[]{:S(2)}, u32[]{:S(2)}) async-start(f32[16,2,4,16,256]{4,3,2,1,0:T(8,128)} %merged.6), calls=%async_computation.3 | async-start | bytes 4194304 | tf_op jit(solution)/shard_map/all_to_all | solution.py:304
  59.7 0.0 collective-permute-done.x_ref
  59.7 5.8 %merged.5 = (f32[16,2,8,8,256]{4,3,2,1,0:T(8,128)}, f32[16,2,8,8,256]{4,3,2,1,0:T(8,128)}) custom-call(s32[1]{0:T(128)} %constant.6.clone.1.start_ref, f32[2,4,256,256]{3,2,1,0:T(8,128)} %collective-permute-done.x_ref, bf16[2,3,2,256,256]{4,3,2,1,0:T(8,128)(2,1)} %prep.1.g_ref, ...), custom_call_target="tpu_custom_call", output_to_operand_aliasing={{0}: (3, {}), {1}: (4, {})} | custom-call | flops 30000001024 | bytes 1 | tf_op jit(solution)/shard_map/merged/pallas_call | solution.py:90
  65.5 21.3 %all-to-all-done.3 = f32[16,2,4,16,256]{4,3,2,1,0:T(8,128)S(1)} async-done(((f32[16,2,4,16,256]{4,3,2,1,0:T(8,128)}), f32[16,2,4,16,256]{4,3,2,1,0:T(8,128)S(1)}, u32[]{:S(2)}, u32[]{:S(2)}) %all-to-all-start.3) | async-done | bytes 2097184 | tf_op jit(solution)/shard_map/all_to_all | solution.py:304
  86.8 0.0 copy-start
  86.8 1.3 copy-done
  88.1 5.8 %all-to-all-start.1 = ((f32[16,2,8,8,256]{4,3,2,1,0:T(8,128)}), f32[16,2,8,8,256]{4,3,2,1,0:T(8,128)S(1)}, u32[]{:S(2)}, u32[]{:S(2)}) async-start(f32[16,2,8,8,256]{4,3,2,1,0:T(8,128)} %get-tuple-element.30), calls=%async_computation.1 | async-start | bytes 4194304 | tf_op jit(solution)/shard_map/all_to_all | solution.py:304
  93.9 0.0 copy-start.1
  93.9 1.6 copy-done.1
  95.5 5.1 %local.3 = f32[2,4,2,2,2,2,16,256]{7,6,5,4,3,2,1,0:T(8,128)} custom-call(f32[96]{0:T(128)S(1)} %reshape.47.gate_ref, f32[2,2,2,2,2,4,16,256]{7,6,5,4,3,2,1,0:T(8,128)S(1)} %bitcast.20), custom_call_target="tpu_custom_call" | custom-call | flops 1 | bytes 1 | tf_op jit(solution)/shard_map/local/pallas_call | solution.py:164
  100.6 2.9 %collective-permute-start.4 = (f32[2,4,256,256]{3,2,1,0:T(8,128)}, f32[2,4,256,256]{3,2,1,0:T(8,128)}, u32[]{:S(2)}, u32[]{:S(2)}) collective-permute-start(f32[2,4,256,256]{3,2,1,0:T(8,128)} %bitcast.11.own_ref), channel_id=1, source_target_pairs={{0,2},{1,3},{2,0},{3,1},{4,6},{5,7},{6,4},{7,5},{8,10},{9,11},{10,... | collective-permute-start | bytes 6291464 | tf_op jit(solution)/shard_map/ppermute | solution.py:301
  103.5 17.5 %all-to-all-done.1 = f32[16,2,8,8,256]{4,3,2,1,0:T(8,128)S(1)} async-done(((f32[16,2,8,8,256]{4,3,2,1,0:T(8,128)}), f32[16,2,8,8,256]{4,3,2,1,0:T(8,128)S(1)}, u32[]{:S(2)}, u32[]{:S(2)}) %all-to-all-start.1) | async-done | bytes 2097184 | tf_op jit(solution)/shard_map/all_to_all | solution.py:304
  120.9 5.8 %all-to-all-start = ((f32[16,2,8,8,256]{4,3,2,1,0:T(8,128)}), f32[16,2,8,8,256]{4,3,2,1,0:T(8,128)}, u32[]{:S(2)}, u32[]{:S(2)}) async-start(f32[16,2,8,8,256]{4,3,2,1,0:T(8,128)} %get-tuple-element.29), calls=%async_computation | async-start | bytes 4194304 | tf_op jit(solution)/shard_map/all_to_all | solution.py:304
  126.8 0.0 collective-permute-done.1.far_ref
  126.8 5.4 %narrow.2 = f32[2,4,4,256,256]{4,3,2,1,0:T(8,128)} custom-call(s32[1]{0:T(128)} %bitcast.bit_ref, f32[96]{0:T(128)S(1)} %reshape.47.gate_ref, f32[2,4,256,256]{3,2,1,0:T(8,128)} %bitcast.6.own_ref, f32[2,4,256,256]{3,2,1,0:T(8,128)} %collective-permute-done.1.far_ref), custom_call_target="tpu_custom_call" | custom-call | flops 49999998976 | bytes 1 | tf_op jit(solution)/shard_map/narrow/pallas_call | solution.py:201
  132.1 5.1 %pair.2 = (f32[2,4,4,2,2,2,2,16,256]{8,7,6,5,4,3,2,1,0:T(8,128)}, f32[2,4,2,2,2,2,8,256]{7,6,5,4,3,2,1,0:T(8,128)S(1)}) custom-call(s32[1]{0:T(128)} %bitcast.bit_ref, f32[96]{0:T(128)S(1)} %reshape.47.gate_ref, f32[2,2,2,2,2,2,4,8,256]{8,7,6,5,4,3,2,1,0:T(8,128)S(1)} %bitcast.18, ...), custom_call_target="tpu_custom_call", output_to_operand_aliasing={{0}: (4, {})} | custom-call | flops 1 | bytes 1 | tf_op jit(solution)/shard_map/pair/pallas_call | solution.py:242
  137.2 2.9 %collective-permute-start.3 = (f32[2,4,16,8,256]{4,3,2,1,0:T(8,128)S(1)}, f32[2,4,16,8,256]{4,3,2,1,0:T(8,128)S(1)}, u32[]{:S(2)}, u32[]{:S(2)}) collective-permute-start(f32[2,4,16,8,256]{4,3,2,1,0:T(8,128)S(1)} %bitcast.22), channel_id=1, source_target_pairs={{0,2},{1,3},{2,0},{3,1},{4,6},{5,7},{6,4},{7,5},{8,10},{9,11},{10,... | collective-permute-start | bytes 3145736 | tf_op jit(solution)/shard_map/ppermute | solution.py:301
  140.1 13.7 %all-to-all-done = f32[16,2,8,8,256]{4,3,2,1,0:T(8,128)} async-done(((f32[16,2,8,8,256]{4,3,2,1,0:T(8,128)}), f32[16,2,8,8,256]{4,3,2,1,0:T(8,128)}, u32[]{:S(2)}, u32[]{:S(2)}) %all-to-all-start) | async-done | bytes 2097184 | tf_op jit(solution)/shard_map/all_to_all | solution.py:304
  153.8 6.1 %pair.3 = (f32[2,4,4,2,2,2,2,16,256]{8,7,6,5,4,3,2,1,0:T(8,128)}, f32[2,4,2,2,2,2,8,256]{7,6,5,4,3,2,1,0:T(8,128)S(1)}) custom-call(s32[1]{0:T(128)} %bitcast.bit_ref, f32[96]{0:T(128)S(1)} %reshape.47.gate_ref, f32[2,2,2,2,2,2,4,8,256]{8,7,6,5,4,3,2,1,0:T(8,128)} %bitcast.3.own_ref.far_ref, ...), custom_call_target="tpu_custom_call", output_to_operand_aliasing={{0}: (4, {})} | custom-call | flops 1 | bytes 1 | tf_op jit(solution)/shard_map/pair/pallas_call | solution.py:242
  159.9 2.9 %collective-permute-start.2 = (f32[2,4,16,8,256]{4,3,2,1,0:T(8,128)S(1)}, f32[2,4,16,8,256]{4,3,2,1,0:T(8,128)S(1)}, u32[]{:S(2)}, u32[]{:S(2)}) collective-permute-start(f32[2,4,16,8,256]{4,3,2,1,0:T(8,128)S(1)} %bitcast.23), channel_id=1, source_target_pairs={{0,2},{1,3},{2,0},{3,1},{4,6},{5,7},{6,4},{7,5},{8,10},{9,11},{10,... | collective-permute-start | bytes 3145736 | tf_op jit(solution)/shard_map/ppermute | solution.py:301
  162.8 0.0 collective-permute-done.4.far_ref
  162.9 5.4 %narrow.3 = f32[2,4,4,256,256]{4,3,2,1,0:T(8,128)} custom-call(s32[1]{0:T(128)} %bitcast.bit_ref, f32[96]{0:T(128)S(1)} %reshape.47.gate_ref, f32[2,4,256,256]{3,2,1,0:T(8,128)} %bitcast.11.own_ref, f32[2,4,256,256]{3,2,1,0:T(8,128)} %collective-permute-done.4.far_ref, f32[2,4,4,256,256]{4,3,2,1,0:T(8,128)} %bitcast.25), custom_call_target="tpu_custom_call", output_to_operand_aliasing={{}: (4, {})} | custom-call | flops 10000000000 | bytes 1 | tf_op jit(solution)/shard_map/narrow/pallas_call | solution.py:201
  168.2 3.7 %collective-permute-done.3.piece_ref = f32[2,4,16,8,256]{4,3,2,1,0:T(8,128)S(1)} collective-permute-done((f32[2,4,16,8,256]{4,3,2,1,0:T(8,128)S(1)}, f32[2,4,16,8,256]{4,3,2,1,0:T(8,128)S(1)}, u32[]{:S(2)}, u32[]{:S(2)}) %collective-permute-start.3) | collective-permute-done | bytes 1048608 | tf_op jit(solution)/shard_map/ppermute | solution.py:301
  171.9 1.6 place.2.held_ref
  173.6 20.9 %collective-permute-done.2.piece_ref = f32[2,4,16,8,256]{4,3,2,1,0:T(8,128)S(1)} collective-permute-done((f32[2,4,16,8,256]{4,3,2,1,0:T(8,128)S(1)}, f32[2,4,16,8,256]{4,3,2,1,0:T(8,128)S(1)}, u32[]{:S(2)}, u32[]{:S(2)}) %collective-permute-start.2) | collective-permute-done | bytes 1048608 | tf_op jit(solution)/shard_map/ppermute | solution.py:301
  194.4 1.6 place.3
Async XLA Ops:
  3.0 56.7 %collective-permute-start = (f32[2,4,256,256]{3,2,1,0:T(8,128)}, f32[2,4,256,256]{3,2,1,0:T(8,128)}, u32[]{:S(2)}, u32[]{:S(2)}) collective-permute-start(f32[2,4,256,256]{3,2,1,0:T(8,128)} %dynamic-slice_bitcast_fusion), channel_id=1, source_target_pairs={{0,2},{1,3},{2,0},{3,1},{4,6},{5,7},{6,4},{7,5},{8,10},{9,11},{10,... | collective-permute-start | bytes 6291464 | tf_op jit(solution)/shard_map/ppermute | solution.py:301
  15.1 33.7 %all-to-all-start.2 = ((f32[16,2,4,16,256]{4,3,2,1,0:T(8,128)}), f32[16,2,4,16,256]{4,3,2,1,0:T(8,128)S(1)}, u32[]{:S(2)}, u32[]{:S(2)}) async-start(f32[16,2,4,16,256]{4,3,2,1,0:T(8,128)} %merged.7), calls=%async_computation.2 | async-start | bytes 4194304 | tf_op jit(solution)/shard_map/all_to_all | solution.py:304
  27.4 5.6 %copy-start.2 = (f32[3,2,4,4]{3,2,1,0:T(4,128)S(1)}, f32[3,2,4,4]{3,2,1,0:T(4,128)}, u32[]{:S(2)}) copy-start(f32[3,2,4,4]{3,2,1,0:T(4,128)} %param.7) | copy-start | bytes 1156
  53.8 73.0 %collective-permute-start.1 = (f32[2,4,256,256]{3,2,1,0:T(8,128)}, f32[2,4,256,256]{3,2,1,0:T(8,128)}, u32[]{:S(2)}, u32[]{:S(2)}) collective-permute-start(f32[2,4,256,256]{3,2,1,0:T(8,128)} %bitcast.6.own_ref), channel_id=1, source_target_pairs={{0,2},{1,3},{2,0},{3,1},{4,6},{5,7},{6,4},{7,5},{8,10},{9,11},{10,... | collective-permute-start | bytes 6291464 | tf_op jit(solution)/shard_map/ppermute | solution.py:301
  53.8 33.0 %all-to-all-start.3 = ((f32[16,2,4,16,256]{4,3,2,1,0:T(8,128)}), f32[16,2,4,16,256]{4,3,2,1,0:T(8,128)S(1)}, u32[]{:S(2)}, u32[]{:S(2)}) async-start(f32[16,2,4,16,256]{4,3,2,1,0:T(8,128)} %merged.6), calls=%async_computation.3 | async-start | bytes 4194304 | tf_op jit(solution)/shard_map/all_to_all | solution.py:304
  86.8 1.3 copy-start
  88.1 32.9 %all-to-all-start.1 = ((f32[16,2,8,8,256]{4,3,2,1,0:T(8,128)}), f32[16,2,8,8,256]{4,3,2,1,0:T(8,128)S(1)}, u32[]{:S(2)}, u32[]{:S(2)}) async-start(f32[16,2,8,8,256]{4,3,2,1,0:T(8,128)} %get-tuple-element.30), calls=%async_computation.1 | async-start | bytes 4194304 | tf_op jit(solution)/shard_map/all_to_all | solution.py:304
  93.9 1.6 copy-start.1
  100.6 62.3 %collective-permute-start.4 = (f32[2,4,256,256]{3,2,1,0:T(8,128)}, f32[2,4,256,256]{3,2,1,0:T(8,128)}, u32[]{:S(2)}, u32[]{:S(2)}) collective-permute-start(f32[2,4,256,256]{3,2,1,0:T(8,128)} %bitcast.11.own_ref), channel_id=1, source_target_pairs={{0,2},{1,3},{2,0},{3,1},{4,6},{5,7},{6,4},{7,5},{8,10},{9,11},{10,... | collective-permute-start | bytes 6291464 | tf_op jit(solution)/shard_map/ppermute | solution.py:301
  120.9 32.9 %all-to-all-start = ((f32[16,2,8,8,256]{4,3,2,1,0:T(8,128)}), f32[16,2,8,8,256]{4,3,2,1,0:T(8,128)}, u32[]{:S(2)}, u32[]{:S(2)}) async-start(f32[16,2,8,8,256]{4,3,2,1,0:T(8,128)} %get-tuple-element.29), calls=%async_computation | async-start | bytes 4194304 | tf_op jit(solution)/shard_map/all_to_all | solution.py:304
  137.2 34.7 %collective-permute-start.3 = (f32[2,4,16,8,256]{4,3,2,1,0:T(8,128)S(1)}, f32[2,4,16,8,256]{4,3,2,1,0:T(8,128)S(1)}, u32[]{:S(2)}, u32[]{:S(2)}) collective-permute-start(f32[2,4,16,8,256]{4,3,2,1,0:T(8,128)S(1)} %bitcast.22), channel_id=1, source_target_pairs={{0,2},{1,3},{2,0},{3,1},{4,6},{5,7},{6,4},{7,5},{8,10},{9,11},{10,... | collective-permute-start | bytes 3145736 | tf_op jit(solution)/shard_map/ppermute | solution.py:301
  159.9 34.5 %collective-permute-start.2 = (f32[2,4,16,8,256]{4,3,2,1,0:T(8,128)S(1)}, f32[2,4,16,8,256]{4,3,2,1,0:T(8,128)S(1)}, u32[]{:S(2)}, u32[]{:S(2)}) collective-permute-start(f32[2,4,16,8,256]{4,3,2,1,0:T(8,128)S(1)} %bitcast.23), channel_id=1, source_target_pairs={{0,2},{1,3},{2,0},{3,1},{4,6},{5,7},{6,4},{7,5},{8,10},{9,11},{10,... | collective-permute-start | bytes 3145736 | tf_op jit(solution)/shard_map/ppermute | solution.py:301

commit v3 on v2

v3 whole, which is shorter than its diff:
```python
import jax
import jax.numpy as jnp
from jax import lax
from jax.experimental import pallas as pl
from jax.experimental.pallas import tpu as pltpu
from jax.sharding import PartitionSpec as P

f32, bf16 = jnp.float32, jnp.bfloat16
G = 256
ROWS = 16
CHUNK = 4
PAIR = 2
RETURNS = ((0, 0, 2), (1, 0, 1), (1, 1, 1))


def cost(weight):
    return pl.CostEstimate(flops=weight, bytes_accessed=1, transcendentals=0)


def params(mib):
    return pltpu.CompilerParams(vmem_limit_bytes=mib << 20)


def hbm(x):
    return pltpu.with_memory_space_constraint(x, pltpu.HBM)


def split(x):
    high = x.astype(bf16)
    return high, (x - high.astype(f32)).astype(bf16)


def prepare(low_ref, mid_ref, g_ref):
    for at, ref in enumerate((low_ref, mid_ref)):
        real, imag = ref[0], ref[1]
        for j, part in enumerate((real, imag - real, real + imag)):
            g_ref[at, j, 0], g_ref[at, j, 1] = split(part)


def merged_kernel(x_ref, g_ref, refs):

    def right(value, j):
        high, low = split(value)
        out = None
        for a, b in ((high, 0), (high, 1), (low, 0)):
            term = lax.dot_general(a, g_ref[0, j, b], (((1,), (1,)), ((), ())), preferred_element_type=f32)
            out = term if out is None else out + term
        return out

    def left(value, j):
        high, low = split(value)
        out = None
        for a, b in ((0, high), (0, low), (1, high)):
            term = jnp.dot(g_ref[1, j, a], b, preferred_element_type=f32)
            out = term if out is None else out + term
        return out

    def both(apply, real, imag):
        shared = apply(real + imag, 0)
        cross = apply(real, 1)
        return shared - apply(imag, 2), shared + cross

    firsts = [both(right, x_ref[0, i], x_ref[1, i]) for i in range(PAIR)]
    for i, first in enumerate(firsts):
        for c, value in enumerate(both(left, *first)):
            value = value.reshape(G // ROWS, ROWS, G)
            for at, o_ref in enumerate(refs):
                rows = ROWS // len(refs)
                o_ref[:, c, i] = value[:, at * rows : (at + 1) * rows]


def merged(x, start, gates, count=CHUNK, parts=1, part=0, held=(), weight=1):
    rows = ROWS // parts
    total = 2 * CHUNK if parts == 2 else count
    out = jax.ShapeDtypeStruct((G // ROWS, 2, total, rows, G), f32)
    spec = pl.BlockSpec((G // ROWS, 2, PAIR, rows, G), lambda i, s: (0, 0, part + i, 0, 0))
    gate = pl.BlockSpec((2, G, G), lambda i, s: (0, 0, 0))

    def kernel(start_ref, x_ref, low_ref, mid_ref, *refs):
        g_ref = refs[-1]

        @pl.when(pl.program_id(0) == 0)
        def _():
            prepare(low_ref, mid_ref, g_ref)

        merged_kernel(x_ref, g_ref, refs[len(held) : -1])

    return pl.pallas_call(
        kernel,
        out_shape=[out] * parts,
        grid_spec=pltpu.PrefetchScalarGridSpec(
            num_scalar_prefetch=1,
            grid=(count // PAIR,),
            in_specs=[pl.BlockSpec((2, PAIR, G, G), lambda i, s: (0, s[0] + i, 0, 0)), gate, gate]
            + [pl.BlockSpec(memory_space=pl.ANY)] * len(held),
            out_specs=[spec] * parts,
            scratch_shapes=[pltpu.VMEM((2, 3, 2, G, G), bf16)],
        ),
        input_output_aliases={4 + j: j for j in range(len(held))},
        cost_estimate=cost(weight),
        compiler_params=params(60),
        name="merged",
    )(start, hbm(x), *gates, *held)


def combine(coef, amps, rows=4):
    outs = []
    for row in range(rows):
        real = imag = None
        for col, (ar, ai) in enumerate(amps):
            cr, ci = coef(row, col)
            real = cr * ar - ci * ai if real is None else real + (cr * ar - ci * ai)
            imag = cr * ai + ci * ar if imag is None else imag + (cr * ai + ci * ar)
        outs.append((real, imag))
    return outs


def plain(gate_ref, k):
    def coef(row, col):
        return gate_ref[32 * k + 4 * row + col], gate_ref[32 * k + 16 + 4 * row + col]

    return coef


def narrow_coef(gate_ref, own):
    bit = (own, 1 - own)

    def coef(row, col):
        at = 64 + 4 * (2 * bit[row >> 1] + (row & 1)) + 2 * bit[col >> 1] + (col & 1)
        return gate_ref[at], gate_ref[at + 16]

    return coef


def wide_high(gate_ref, ref, out):
    for w0 in range(2):
        for h0 in range(2):
            where = [(w2, w0, 2 * h1 + h0) for w2 in range(2) for h1 in range(2)]
            amps = [(ref[a, b, 0, h], ref[a, b, 1, h]) for a, b, h in where]
            for (a, b, h), (real, imag) in zip(where, combine(plain(gate_ref, 1), amps)):
                out[a, b, 0, h], out[a, b, 1, h] = real, imag


def wide_low(gate_ref, ref, w2, h1):
    where = [(w0, h0) for w0 in range(2) for h0 in range(2)]
    amps = [(ref[w2, w0, 0, 2 * h1 + h0], ref[w2, w0, 1, 2 * h1 + h0]) for w0, h0 in where]
    return dict(zip(where, combine(plain(gate_ref, 0), amps)))


def local_kernel(gate_ref, x_ref, o_ref):
    for w1 in range(2):
        for w2 in range(2):
            for h1 in range(x_ref.shape[4] // 2):
                for (w0, h0), (real, imag) in wide_low(gate_ref, x_ref.at[:, w1], w2, h1).items():
                    o_ref[0, 2 * h1 + h0, w2, w1, w0] = real
                    o_ref[1, 2 * h1 + h0, w2, w1, w0] = imag


def local(gates, x):
    count = x.shape[2]
    return pl.pallas_call(
        local_kernel,
        out_shape=jax.ShapeDtypeStruct((2, count, 2, 2, 2, 2, ROWS, G), f32),
        grid_spec=pltpu.PrefetchScalarGridSpec(
            num_scalar_prefetch=1,
            grid=(2,),
            in_specs=[pl.BlockSpec((None, 2, 2, 2, 2, count, ROWS, G), lambda i, g: (i, 0, 0, 0, 0, 0, 0, 0))],
            out_specs=pl.BlockSpec((2, count, None, 2, 2, 2, ROWS, G), lambda i, g: (0, 0, i, 0, 0, 0, 0, 0)),
        ),
        cost_estimate=cost(1),
        compiler_params=params(16),
        name="local",
    )(gates, x.reshape(2, 2, 2, 2, 2, count, ROWS, G)).reshape(2, count, G, G)


def narrow_kernel(gate_ref, own, sources, out_ref, scratch):
    coef = narrow_coef(gate_ref, own)
    per = len(sources[0])
    for w2 in range(2):
        for w0 in range(2):
            for h1 in range(2):
                amps = []
                for refs in sources:
                    ref = refs[h1 * per // 2]
                    for h0 in range(2):
                        h = h0 if per == 2 else 2 * h1 + h0
                        amps.append((ref[0, h, w2, w0], ref[1, h, w2, w0]))
                for h0, (real, imag) in enumerate(combine(coef, amps, 2)):
                    scratch[w2, w0, 0, 2 * h1 + h0] = real
                    scratch[w2, w0, 1, 2 * h1 + h0] = imag
    for w0 in range(2):
        for h0 in range(2):
            where = [(w2, w0, 2 * h1 + h0) for w2 in range(2) for h1 in range(2)]
            amps = [(scratch[a, b, 0, h], scratch[a, b, 1, h]) for a, b, h in where]
            for (a, b, h), (real, imag) in zip(where, combine(plain(gate_ref, 1), amps)):
                out_ref[0, h, a, b], out_ref[1, h, a, b] = real, imag


def narrow(bit, gates, own, far, group, held, weight=1):
    per = len(own)
    count = CHUNK // per
    source = pl.BlockSpec((2, count, None, 2, None, 2, ROWS, G), lambda i, j, s, g: (0, 0, i, 0, j, 0, 0, 0))
    full = (2, 4, CHUNK, 2, 2, 2, 2, ROWS, G)
    extra = [] if held is None else [held.reshape(full)]

    def kernel(bit_ref, gate_ref, *refs):
        narrow_kernel(gate_ref, bit_ref[0], (refs[:per], refs[per : 2 * per]), refs[-2], refs[-1])

    return pl.pallas_call(
        kernel,
        out_shape=jax.ShapeDtypeStruct(full, f32),
        grid_spec=pltpu.PrefetchScalarGridSpec(
            num_scalar_prefetch=2,
            grid=(2, 2),
            in_specs=[source] * (2 * per) + [pl.BlockSpec(memory_space=pl.ANY)] * len(extra),
            out_specs=pl.BlockSpec(
                (2, None, CHUNK, None, 2, None, 2, ROWS, G), lambda i, j, s, g: (0, group, 0, i, 0, j, 0, 0, 0)
            ),
            scratch_shapes=[pltpu.VMEM((2, 2, 2, CHUNK, ROWS, G), f32)],
        ),
        input_output_aliases={2 + 2 * per: 0} if extra else {},
        cost_estimate=cost(weight),
        compiler_params=params(16),
        name="narrow",
    )(bit, gates, *(value.reshape(2, count, 2, 2, 2, 2, ROWS, G) for value in (*own, *far)), *extra)


def pair_kernel(bit_ref, gate_ref, own_ref, far_ref, held_ref, out_ref, back_ref, scratch):
    for n, ref in enumerate((own_ref, far_ref)):
        wide_high(gate_ref, ref, scratch.at[n])
    coef = narrow_coef(gate_ref, bit_ref[0])
    for w2 in range(2):
        for h1 in range(2):
            state = [wide_low(gate_ref, scratch.at[n], w2, h1) for n in range(2)]
            for w0 in range(2):
                where = [(n, h0) for n in range(2) for h0 in range(2)]
                values = combine(coef, [state[n][w0, h0] for n, h0 in where])
                for (n, h0), (real, imag) in zip(where, values):
                    target = (out_ref, back_ref)[n]
                    target[0, 2 * h1 + h0, w2, w0] = real
                    target[1, 2 * h1 + h0, w2, w0] = imag


def pair(bit, gates, both, half, first, count, held):
    def source(part):
        return pl.BlockSpec(
            (None, 2, None, 2, 2, None, CHUNK, 8, G), lambda i, j, s, g: (first + i, 0, j, 0, 0, part, 0, 0, 0)
        )

    both = both.reshape(2, 2, 2, 2, 2, 2, CHUNK, 8, G)
    full = (2, 4, CHUNK, 2, 2, 2, 2, ROWS, G)
    back = (2, CHUNK, count, 2, 2, 2, 8, G)
    held, back = pl.pallas_call(
        pair_kernel,
        out_shape=[jax.ShapeDtypeStruct(full, f32), jax.ShapeDtypeStruct(back, f32)],
        grid_spec=pltpu.PrefetchScalarGridSpec(
            num_scalar_prefetch=2,
            grid=(count, 2),
            in_specs=[source(0), source(1), pl.BlockSpec(memory_space=pl.ANY)],
            out_specs=[
                pl.BlockSpec(
                    (2, None, CHUNK, None, 2, None, 2, 8, G),
                    lambda i, j, s, g: (0, 2 * s[0], 0, first + i, 0, j, 0, half, 0),
                ),
                pl.BlockSpec((2, CHUNK, None, 2, None, 2, 8, G), lambda i, j, s, g: (0, 0, i, 0, j, 0, 0, 0)),
            ],
            scratch_shapes=[pltpu.VMEM((2, 2, 2, 2, CHUNK, 8, G), f32)],
        ),
        input_output_aliases={4: 0},
        cost_estimate=cost(1),
        compiler_params=params(16),
        name="pair",
    )(bit, gates, both, both, held.reshape(full))
    return held, back.reshape(2, CHUNK, 8 * count, 8, G)


def place_kernel(bit_ref, piece_ref, held_ref, out_ref):
    out_ref[...] = piece_ref[...]


def place(bit, piece, half, first, held, weight=1):
    full = (2, 4, CHUNK, G // ROWS, ROWS, G)
    wide = piece.shape[2]
    return pl.pallas_call(
        place_kernel,
        out_shape=jax.ShapeDtypeStruct(full, f32),
        grid_spec=pltpu.PrefetchScalarGridSpec(
            num_scalar_prefetch=1,
            grid=(CHUNK // 2,),
            in_specs=[
                pl.BlockSpec((2, 2, wide, 8, G), lambda h, s: (0, h, 0, 0, 0)),
                pl.BlockSpec(memory_space=pl.ANY),
            ],
            out_specs=pl.BlockSpec(
                (2, None, 2, wide, 8, G), lambda h, s: (0, 2 * (1 - s[0]), h, first, half, 0)
            ),
        ),
        input_output_aliases={2: 0},
        cost_estimate=cost(weight),
        compiler_params=params(16),
        name="place",
    )(bit, piece, held.reshape(full))


def body(amplitudes, low_gate, mid_gate, pair_gates):
    x = amplitudes.reshape(2, 16, G, G)
    bit = lax.axis_index("narrow") >> 1 & 1
    bits = bit.reshape(1).astype(jnp.int32)
    partners = [(i, i ^ 2) for i in range(lax.axis_size("narrow"))]
    barrier = lax.optimization_barrier

    def swapped(value):
        return lax.ppermute(value, "narrow", partners)

    def remap(value):
        return lax.all_to_all(value, "wide", split_axis=0, concat_axis=0, tiled=True)

    def group(value):
        return jnp.full((1,), value, jnp.int32)


    def piece(bit, part):
        return lax.dynamic_slice_in_dim(x, 8 * (1 - bit) + PAIR * part, PAIR, 1)

    flat = pair_gates.reshape(96)
    bits, low_gate, sent = barrier((bits, low_gate, piece(bit, 0)))
    arrived = [swapped(sent)]
    gates = (low_gate, mid_gate)
    early = merged(x, group(2), gates, PAIR)[0]
    later, low_gate, early = barrier((bits, low_gate, early))
    arrived.append(swapped(piece(later[0], 1)))
    gates = (low_gate, mid_gate)
    late = merged(x, group(3), gates, PAIR)[0]
    own = merged(x, 4 * later, gates, CHUNK, 2, 0)
    first = [local(flat, remap(early))]
    own, late, low_gate, first[0] = barrier((own, late, low_gate, first[0]))
    second = merged(x, group(6), (low_gate, mid_gate))[0]
    first.append(local(flat, remap(late)))
    second = local(flat, remap(second))
    both = own
    distant = [swapped(value) for value in first]
    arrived[1], distant[0] = barrier((arrived[1], distant[0]))
    for part in range(2):
        both = merged(arrived[part], group(0), gates, PAIR, 2, 2 + part, both, (30000000000, 30000000000)[part])
    held = narrow(bits, flat, first, distant, 1, None, 20000000000)
    both = list(both)
    both[1], held = barrier((both[1], held))
    both[0], second = barrier((both[0], second))
    front, rest = remap(both[0]), remap(both[1])
    backs = []
    for half, first_wide, count in RETURNS:
        held, back = pair(bits, flat, (front, rest)[half], half, first_wide, count, held)
        backs.append(swapped(back))
        if half == 0:
            held = narrow(bits, flat, [second], [swapped(second)], 3, held, 25000000000)
    for back, (half, first_wide, _) in zip(backs, RETURNS):
        held = place(bits, back, half, first_wide, held, 1000000000)
    return held.reshape(amplitudes.shape)


def solution(mesh):
    in_specs = (P(None, "wide", "narrow", None, None, None), P(), P(), P())
    out_specs = P(None, "wide", "narrow", None, None, None)
    return jax.shard_map(body, mesh=mesh, in_specs=in_specs, out_specs=out_specs, check_vma=False)
```

time: 197 us -> 190 us (0.964); the launches traced: 196 us -> 187 us
  waiting for transfers between devices: 92.6 us -> 79.7 us
  starting transfers between devices: 36.7 us -> 39.9 us
    all_to_all x4 -> x5, waiting for transfers between devices: 68.1 us -> 51.1 us  [remap(): lax.all_to_all(value, 'wide', split_axis=0, concat_axis=0, tiled=True)]
    pallas_call x5, Pallas kernels: 23.5 us -> 18.1 us  [the longest x2 11.5 us: narrow(): pl.pallas_call(kernel, out_shape=jax.ShapeDtypeStruct(full, f32), grid_sp...]
    pallas_call x4 -> x6, Pallas kernels: 22.7 us -> 27.5 us  [merged(): pl.pallas_call(kernel, out_shape=[out] * parts, grid_spec=pltpu.PrefetchS...]
    ppermute x5 -> x8, waiting for transfers between devices: 24.6 us -> 28.5 us  [swapped(): return lax.ppermute(value, 'narrow', partners)]
    all_to_all x4 -> x5, starting transfers between devices: 24.2 us -> 28.1 us  [remap(): lax.all_to_all(value, 'wide', split_axis=0, concat_axis=0, tiled=True)]
    ppermute x5 -> x8, starting transfers between devices: 12.5 us -> 11.8 us  [swapped(): return lax.ppermute(value, 'narrow', partners)]
    pallas_call x2 -> x3, Pallas kernels: 11.2 us -> 11.4 us  [pair(): pl.pallas_call(pair_kernel, out_shape=[jax.ShapeDtypeStruct(full, f32), j...]
  transfers between devices with their start and end apart: 9 -> 13, of which waited for: 6 -> 9; matrix products, arithmetic and copies ran while one was open for 0% -> 1% of each run, Pallas kernels for 30% -> 32%
where the time goes in v3:
time: 190 us; the launch traced here: 187 us
  waiting for transfers between devices  79.7 us (42%)
  Pallas kernels  59.8 us (31%)
  starting transfers between devices  39.9 us (21%)
  local copies, waits for them, and re-layouts  7.56 us (4%)
    all_to_all x5, waiting for transfers between devices, remap(): lax.all_to_all(value, 'wide', split_axis=0, concat_axis=0, tiled=True)  51.1 us
    ppermute x8, waiting for transfers between devices, swapped(): return lax.ppermute(value, 'narrow', partners)  28.5 us
    all_to_all x5, starting transfers between devices, remap(): lax.all_to_all(value, 'wide', split_axis=0, concat_axis=0, tiled=True)  28.1 us
    pallas_call x6, Pallas kernels, merged(): pl.pallas_call(kernel, out_shape=[out] * parts, grid_spec=pltpu.PrefetchS...  27.5 us
    ppermute x8, starting transfers between devices, swapped(): return lax.ppermute(value, 'narrow', partners)  11.8 us
    pallas_call x2, Pallas kernels, narrow(): pl.pallas_call(kernel, out_shape=jax.ShapeDtypeStruct(full, f32), grid_sp...  11.5 us
    pallas_call x3, Pallas kernels, pair(): pl.pallas_call(pair_kernel, out_shape=[jax.ShapeDtypeStruct(full, f32), j...  11.4 us
    pallas_call x3, Pallas kernels, local(): pl.pallas_call(local_kernel, out_shape=jax.ShapeDtypeStruct((2, count, 2,...  6.59 us
  transfers between devices with their start and end apart: 13, of which 9 were waited for; matrix products, arithmetic and copies ran while one was open for 1% of the time, Pallas kernels for 32%

profile of v3, /device:TPU:1, one launch (start us, length us, event | category | flops | bytes accessed | tf_op | source)
XLA Modules:
  0.0 187.0 jit_solution(6520952511319213788)
XLA Ops:
  0.0 1.3 dynamic-slice_bitcast_fusion.1
  1.3 3.8 %collective-permute-start.2 = (f32[2,2,256,256]{3,2,1,0:T(8,128)S(1)}, f32[2,2,256,256]{3,2,1,0:T(8,128)S(1)}, u32[]{:S(2)}, u32[]{:S(2)}) collective-permute-start(f32[2,2,256,256]{3,2,1,0:T(8,128)S(1)} %dynamic-slice_bitcast_fusion.1), channel_id=1, source_target_pairs={{0,2},{1,3},{2,0},{3,1},{4,6},{5,7},{6,4},{7,5},{8,10},{9,11},{10,... | collective-permute-start | bytes 3145736 | tf_op jit(solution)/shard_map/ppermute | solution.py:313
  5.1 3.9 %merged.6 = f32[16,2,2,16,256]{4,3,2,1,0:T(8,128)} custom-call(s32[1]{0:T(128)} %constant.27.clone.1.start_ref, f32[2,16,256,256]{3,2,1,0:T(8,128)} %bitcast.41, f32[2,256,256]{2,1,0:T(8,128)} %low_ref.5, f32[2,256,256]{2,1,0:T(8,128)} %mid_ref.11), custom_call_target="tpu_custom_call" | custom-call | flops 1 | bytes 1 | tf_op jit(solution)/shard_map/merged/pallas_call | solution.py:88
  9.1 6.6 %all-to-all-start = ((f32[16,2,2,16,256]{4,3,2,1,0:T(8,128)}), f32[16,2,2,16,256]{4,3,2,1,0:T(8,128)S(1)}, u32[]{:S(2)}, u32[]{:S(2)}) async-start(f32[16,2,2,16,256]{4,3,2,1,0:T(8,128)} %merged.6), calls=%async_computation | async-start | bytes 2097152 | tf_op jit(solution)/shard_map/all_to_all | solution.py:316
  15.7 2.3 %dynamic-slice_bitcast_fusion = f32[2,2,256,256]{3,2,1,0:T(8,128)} fusion(f32[2,1,1,16,256,256]{5,4,3,2,1,0:T(8,128)} %param.4, s32[]{:T(128)S(6)} %select_n.7), kind=kLoop, calls=%fused_computation | loop fusion | bytes 2097156 | tf_op jit(solution)/shard_map/dynamic_slice | solution.py:323
  18.0 0.1 collective-permute-start
  18.1 5.8 %merged.7 = (f32[16,2,8,8,256]{4,3,2,1,0:T(8,128)}, f32[16,2,8,8,256]{4,3,2,1,0:T(8,128)}) custom-call(s32[1]{0:T(128)S(6)} %mul.12.start_ref, f32[2,16,256,256]{3,2,1,0:T(8,128)} %bitcast.42, f32[2,256,256]{2,1,0:T(8,128)} %low_ref.5, f32[2,256,256]{2,1,0:T(8,128)} %mid_ref.11), custom_call_target="tpu_custom_call" | custom-call | flops 1 | bytes 1 | tf_op jit(solution)/shard_map/merged/pallas_call | solution.py:88
  23.8 4.0 %merged.8 = f32[16,2,2,16,256]{4,3,2,1,0:T(8,128)} custom-call(s32[1]{0:T(128)} %constant.31.clone.1.start_ref, f32[2,16,256,256]{3,2,1,0:T(8,128)} %bitcast.43, f32[2,256,256]{2,1,0:T(8,128)} %low_ref.5, f32[2,256,256]{2,1,0:T(8,128)} %mid_ref.11), custom_call_target="tpu_custom_call" | custom-call | flops 1 | bytes 1 | tf_op jit(solution)/shard_map/merged/pallas_call | solution.py:88
  27.8 0.1 reshape.75.gate_ref
  27.9 3.6 %all-to-all-done = f32[16,2,2,16,256]{4,3,2,1,0:T(8,128)S(1)} async-done(((f32[16,2,2,16,256]{4,3,2,1,0:T(8,128)}), f32[16,2,2,16,256]{4,3,2,1,0:T(8,128)S(1)}, u32[]{:S(2)}, u32[]{:S(2)}) %all-to-all-start) | async-done | bytes 1048608 | tf_op jit(solution)/shard_map/all_to_all | solution.py:316
  31.5 2.0 %local.3 = f32[2,2,2,2,2,2,16,256]{7,6,5,4,3,2,1,0:T(8,128)} custom-call(f32[96]{0:T(128)S(1)} %reshape.75.gate_ref, f32[2,2,2,2,2,2,16,256]{7,6,5,4,3,2,1,0:T(8,128)S(1)} %bitcast.35), custom_call_target="tpu_custom_call" | custom-call | flops 1 | bytes 1 | tf_op jit(solution)/shard_map/local/pallas_call | solution.py:161
  33.5 0.0 collective-permute-start.1
  33.5 5.6 %all-to-all-start.1 = ((f32[16,2,2,16,256]{4,3,2,1,0:T(8,128)}), f32[16,2,2,16,256]{4,3,2,1,0:T(8,128)S(1)}, u32[]{:S(2)}, u32[]{:S(2)}) async-start(f32[16,2,2,16,256]{4,3,2,1,0:T(8,128)} %merged.8), calls=%async_computation.1 | async-start | bytes 2097152 | tf_op jit(solution)/shard_map/all_to_all | solution.py:316
  39.0 5.7 %merged.11 = f32[16,2,4,16,256]{4,3,2,1,0:T(8,128)} custom-call(s32[1]{0:T(128)} %constant.32.clone.1.start_ref, f32[2,16,256,256]{3,2,1,0:T(8,128)} %bitcast.44, f32[2,256,256]{2,1,0:T(8,128)} %low_ref.5, f32[2,256,256]{2,1,0:T(8,128)} %mid_ref.11), custom_call_target="tpu_custom_call" | custom-call | flops 1 | bytes 1 | tf_op jit(solution)/shard_map/merged/pallas_call | solution.py:88
  44.7 0.0 collective-permute-done.2.x_ref
  44.7 1.0 copy-done.3
  45.7 4.0 %merged.9 = (f32[16,2,8,8,256]{4,3,2,1,0:T(8,128)}, f32[16,2,8,8,256]{4,3,2,1,0:T(8,128)}) custom-call(s32[1]{0:T(128)} %constant.25.clone.1.start_ref, f32[2,2,256,256]{3,2,1,0:T(8,128)} %copy-done.3, f32[2,256,256]{2,1,0:T(8,128)} %low_ref.5, f32[2,256,256]{2,1,0:T(8,128)} %mid_ref.11, ...), custom_call_target="tpu_custom_call", output_to_operand_aliasing={{0}: (4, {}), {1}: (5, {})} | custom-call | flops 30000001024 | bytes 1 | tf_op jit(solution)/shard_map/merged/pallas_call | solution.py:88
  49.7 5.1 %all-to-all-done.1 = f32[16,2,2,16,256]{4,3,2,1,0:T(8,128)S(1)} async-done(((f32[16,2,2,16,256]{4,3,2,1,0:T(8,128)}), f32[16,2,2,16,256]{4,3,2,1,0:T(8,128)S(1)}, u32[]{:S(2)}, u32[]{:S(2)}) %all-to-all-start.1) | async-done | bytes 1048608 | tf_op jit(solution)/shard_map/all_to_all | solution.py:316
  54.9 4.3 %all-to-all-start.3 = ((f32[16,2,4,16,256]{4,3,2,1,0:T(8,128)}), f32[16,2,4,16,256]{4,3,2,1,0:T(8,128)S(1)}, u32[]{:S(2)}, u32[]{:S(2)}) async-start(f32[16,2,4,16,256]{4,3,2,1,0:T(8,128)} %merged.11), calls=%async_computation.3 | async-start | bytes 4194304 | tf_op jit(solution)/shard_map/all_to_all | solution.py:316
  59.1 1.9 %local.4.refs_1_ = f32[2,2,2,2,2,2,16,256]{7,6,5,4,3,2,1,0:T(8,128)} custom-call(f32[96]{0:T(128)S(1)} %reshape.75.gate_ref, f32[2,2,2,2,2,2,16,256]{7,6,5,4,3,2,1,0:T(8,128)S(1)} %bitcast.36), custom_call_target="tpu_custom_call" | custom-call | flops 1 | bytes 1 | tf_op jit(solution)/shard_map/local/pallas_call | solution.py:161
  61.1 2.0 %collective-permute-start.3 = (f32[2,2,256,256]{3,2,1,0:T(8,128)}, f32[2,2,256,256]{3,2,1,0:T(8,128)S(1)}, u32[]{:S(2)}, u32[]{:S(2)}) collective-permute-start(f32[2,2,256,256]{3,2,1,0:T(8,128)} %bitcast.11), channel_id=1, source_target_pairs={{0,2},{1,3},{2,0},{3,1},{4,6},{5,7},{6,4},{7,5},{8,10},{9,11},{10,... | collective-permute-start | bytes 3145736 | tf_op jit(solution)/shard_map/ppermute | solution.py:313
  63.0 0.0 collective-permute-done.x_ref
  63.0 9.7 %collective-permute-done.1 = f32[2,2,256,256]{3,2,1,0:T(8,128)} collective-permute-done((f32[2,2,256,256]{3,2,1,0:T(8,128)}, f32[2,2,256,256]{3,2,1,0:T(8,128)}, u32[]{:S(2)}, u32[]{:S(2)}) %collective-permute-start.1) | collective-permute-done | bytes 1048608 | tf_op jit(solution)/shard_map/ppermute | solution.py:313
  72.8 4.1 %merged.10 = (f32[16,2,8,8,256]{4,3,2,1,0:T(8,128)}, f32[16,2,8,8,256]{4,3,2,1,0:T(8,128)}) custom-call(s32[1]{0:T(128)} %constant.25.clone.1.start_ref, f32[2,2,256,256]{3,2,1,0:T(8,128)} %collective-permute-done.x_ref, f32[2,256,256]{2,1,0:T(8,128)} %low_ref.5, f32[2,256,256]{2,1,0:T(8,128)} %mid_ref.11, ...), custom_call_target="tpu_custom_call", output_to_operand_aliasing={{0}: (4, {}), {1}: (5, {})} | custom-call | flops 30000001024 | bytes 1 | tf_op jit(solution)/shard_map/merged/pallas_call | solution.py:88
  76.9 9.3 %all-to-all-done.3 = f32[16,2,4,16,256]{4,3,2,1,0:T(8,128)S(1)} async-done(((f32[16,2,4,16,256]{4,3,2,1,0:T(8,128)}), f32[16,2,4,16,256]{4,3,2,1,0:T(8,128)S(1)}, u32[]{:S(2)}, u32[]{:S(2)}) %all-to-all-start.3) | async-done | bytes 2097184 | tf_op jit(solution)/shard_map/all_to_all | solution.py:316
  86.2 2.7 %local.5 = f32[2,4,2,2,2,2,16,256]{7,6,5,4,3,2,1,0:T(8,128)} custom-call(f32[96]{0:T(128)S(1)} %reshape.75.gate_ref, f32[2,2,2,2,2,4,16,256]{7,6,5,4,3,2,1,0:T(8,128)S(1)} %bitcast.34), custom_call_target="tpu_custom_call" | custom-call | flops 1 | bytes 1 | tf_op jit(solution)/shard_map/local/pallas_call | solution.py:161
  88.8 2.0 %collective-permute-start.4 = (f32[2,4,256,256]{3,2,1,0:T(8,128)}, f32[2,4,256,256]{3,2,1,0:T(8,128)}, u32[]{:S(2)}, u32[]{:S(2)}) collective-permute-start(f32[2,4,256,256]{3,2,1,0:T(8,128)} %bitcast.15), channel_id=1, source_target_pairs={{0,2},{1,3},{2,0},{3,1},{4,6},{5,7},{6,4},{7,5},{8,10},{9,11},{10,... | collective-permute-start | bytes 6291464 | tf_op jit(solution)/shard_map/ppermute | solution.py:313
  90.8 5.8 %all-to-all-start.4 = ((f32[16,2,8,8,256]{4,3,2,1,0:T(8,128)}), f32[16,2,8,8,256]{4,3,2,1,0:T(8,128)S(1)}, u32[]{:S(2)}, u32[]{:S(2)}) async-start(f32[16,2,8,8,256]{4,3,2,1,0:T(8,128)} %get-tuple-element.55), calls=%async_computation.4 | async-start | bytes 4194304 | tf_op jit(solution)/shard_map/all_to_all | solution.py:316
  96.6 0.0 collective-permute-done.3
  96.6 5.7 %narrow.2.held_ref = f32[2,4,4,2,2,2,2,16,256]{8,7,6,5,4,3,2,1,0:T(8,128)} custom-call(s32[1]{0:T(128)} %bitcast.bit_ref, f32[96]{0:T(128)S(1)} %reshape.75.gate_ref, f32[2,2,2,2,2,2,16,256]{7,6,5,4,3,2,1,0:T(8,128)} %bitcast.8.refs_0_, f32[2,2,2,2,2,2,16,256]{7,6,5,4,3,2,1,0:T(8,128)} %local.4.refs_1_, f32[2,2,2,2,2,2,16,256]{7,6,5,4,3,2,1,0:T(8,128)} %bitcast.10.refs_2_, ...), custom_call_target="tpu_custom_call" | custom-call | flops 20000000000 | bytes 1 | tf_op jit(solution)/shard_map/narrow/pallas_call | solution.py:209
  102.3 21.4 %all-to-all-done.4 = f32[16,2,8,8,256]{4,3,2,1,0:T(8,128)S(1)} async-done(((f32[16,2,8,8,256]{4,3,2,1,0:T(8,128)}), f32[16,2,8,8,256]{4,3,2,1,0:T(8,128)S(1)}, u32[]{:S(2)}, u32[]{:S(2)}) %all-to-all-start.4) | async-done | bytes 2097184 | tf_op jit(solution)/shard_map/all_to_all | solution.py:316
  123.6 1.4 copy-done
  125.0 5.8 %all-to-all-start.2 = ((f32[16,2,8,8,256]{4,3,2,1,0:T(8,128)}), f32[16,2,8,8,256]{4,3,2,1,0:T(8,128)S(1)}, u32[]{:S(2)}, u32[]{:S(2)}) async-start(f32[16,2,8,8,256]{4,3,2,1,0:T(8,128)} %get-tuple-element.51), calls=%async_computation.2 | async-start | bytes 4194304 | tf_op jit(solution)/shard_map/all_to_all | solution.py:316
  130.8 1.6 copy-done.1
  132.4 5.2 %pair.3 = (f32[2,4,4,2,2,2,2,16,256]{8,7,6,5,4,3,2,1,0:T(8,128)}, f32[2,4,2,2,2,2,8,256]{7,6,5,4,3,2,1,0:T(8,128)}) custom-call(s32[1]{0:T(128)} %bitcast.bit_ref, f32[96]{0:T(128)S(1)} %reshape.75.gate_ref, f32[2,2,2,2,2,2,4,8,256]{8,7,6,5,4,3,2,1,0:T(8,128)S(1)} %bitcast.32, ...), custom_call_target="tpu_custom_call", output_to_operand_aliasing={{0}: (4, {})} | custom-call | flops 1 | bytes 1 | tf_op jit(solution)/shard_map/pair/pallas_call | solution.py:253
  137.6 1.0 collective-permute-start.7
  138.6 1.6 collective-permute-done.4
  140.2 5.8 %narrow.3.held_ref = f32[2,4,4,2,2,2,2,16,256]{8,7,6,5,4,3,2,1,0:T(8,128)} custom-call(s32[1]{0:T(128)} %bitcast.bit_ref, f32[96]{0:T(128)S(1)} %reshape.75.gate_ref, f32[2,4,2,2,2,2,16,256]{7,6,5,4,3,2,1,0:T(8,128)} %bitcast.16.refs_0_, f32[2,4,2,2,2,2,16,256]{7,6,5,4,3,2,1,0:T(8,128)} %bitcast.17.refs_1_, ...), custom_call_target="tpu_custom_call", output_to_operand_aliasing={{}: (4, {})} | custom-call | flops 24999999488 | bytes 1 | tf_op jit(solution)/shard_map/narrow/pallas_call | solution.py:209
  146.0 11.8 %all-to-all-done.2 = f32[16,2,8,8,256]{4,3,2,1,0:T(8,128)S(1)} async-done(((f32[16,2,8,8,256]{4,3,2,1,0:T(8,128)}), f32[16,2,8,8,256]{4,3,2,1,0:T(8,128)S(1)}, u32[]{:S(2)}, u32[]{:S(2)}) %all-to-all-start.2) | async-done | bytes 2097184 | tf_op jit(solution)/shard_map/all_to_all | solution.py:316
  157.8 3.1 %pair.4 = (f32[2,4,4,2,2,2,2,16,256]{8,7,6,5,4,3,2,1,0:T(8,128)}, f32[2,4,1,2,2,2,8,256]{7,6,5,4,3,2,1,0:T(8,128)S(1)}) custom-call(s32[1]{0:T(128)} %bitcast.bit_ref, f32[96]{0:T(128)S(1)} %reshape.75.gate_ref, f32[2,2,2,2,2,2,4,8,256]{8,7,6,5,4,3,2,1,0:T(8,128)S(1)} %bitcast.28, ...), custom_call_target="tpu_custom_call", output_to_operand_aliasing={{0}: (4, {})} | custom-call | flops 1 | bytes 1 | tf_op jit(solution)/shard_map/pair/pallas_call | solution.py:253
  160.9 1.0 collective-permute-start.6
  161.9 3.1 %pair.5 = (f32[2,4,4,2,2,2,2,16,256]{8,7,6,5,4,3,2,1,0:T(8,128)}, f32[2,4,1,2,2,2,8,256]{7,6,5,4,3,2,1,0:T(8,128)S(1)}) custom-call(s32[1]{0:T(128)} %bitcast.bit_ref, f32[96]{0:T(128)S(1)} %reshape.75.gate_ref, f32[2,2,2,2,2,2,4,8,256]{8,7,6,5,4,3,2,1,0:T(8,128)S(1)} %bitcast.30, ...), custom_call_target="tpu_custom_call", output_to_operand_aliasing={{0}: (4, {})} | custom-call | flops 1 | bytes 1 | tf_op jit(solution)/shard_map/pair/pallas_call | solution.py:253
  165.0 2.0 %collective-permute-start.5 = (f32[2,4,8,8,256]{4,3,2,1,0:T(8,128)S(1)}, f32[2,4,8,8,256]{4,3,2,1,0:T(8,128)S(1)}, u32[]{:S(2)}, u32[]{:S(2)}) collective-permute-start(f32[2,4,8,8,256]{4,3,2,1,0:T(8,128)S(1)} %bitcast.39), channel_id=1, source_target_pairs={{0,2},{1,3},{2,0},{3,1},{4,6},{5,7},{6,4},{7,5},{8,10},{9,11},{10,... | collective-permute-start | bytes 1572872 | tf_op jit(solution)/shard_map/ppermute | solution.py:313
  167.0 1.1 place.3.held_ref
  168.1 6.8 %collective-permute-done.6.piece_ref = f32[2,4,8,8,256]{4,3,2,1,0:T(8,128)S(1)} collective-permute-done((f32[2,4,8,8,256]{4,3,2,1,0:T(8,128)S(1)}, f32[2,4,8,8,256]{4,3,2,1,0:T(8,128)S(1)}, u32[]{:S(2)}, u32[]{:S(2)}) %collective-permute-start.6) | collective-permute-done | bytes 524320 | tf_op jit(solution)/shard_map/ppermute | solution.py:313
  174.9 0.9 place.4.held_ref
  175.8 10.4 %collective-permute-done.5.piece_ref = f32[2,4,8,8,256]{4,3,2,1,0:T(8,128)S(1)} collective-permute-done((f32[2,4,8,8,256]{4,3,2,1,0:T(8,128)S(1)}, f32[2,4,8,8,256]{4,3,2,1,0:T(8,128)S(1)}, u32[]{:S(2)}, u32[]{:S(2)}) %collective-permute-start.5) | collective-permute-done | bytes 524320 | tf_op jit(solution)/shard_map/ppermute | solution.py:313
  186.1 0.9 place.5
  (6 shorter events, 0.0 us)
Async XLA Ops:
  1.3 43.4 %collective-permute-start.2 = (f32[2,2,256,256]{3,2,1,0:T(8,128)S(1)}, f32[2,2,256,256]{3,2,1,0:T(8,128)S(1)}, u32[]{:S(2)}, u32[]{:S(2)}) collective-permute-start(f32[2,2,256,256]{3,2,1,0:T(8,128)S(1)} %dynamic-slice_bitcast_fusion.1), channel_id=1, source_target_pairs={{0,2},{1,3},{2,0},{3,1},{4,6},{5,7},{6,4},{7,5},{8,10},{9,11},{10,... | collective-permute-start | bytes 3145736 | tf_op jit(solution)/shard_map/ppermute | solution.py:313
  9.1 22.4 %all-to-all-start = ((f32[16,2,2,16,256]{4,3,2,1,0:T(8,128)}), f32[16,2,2,16,256]{4,3,2,1,0:T(8,128)S(1)}, u32[]{:S(2)}, u32[]{:S(2)}) async-start(f32[16,2,2,16,256]{4,3,2,1,0:T(8,128)} %merged.6), calls=%async_computation | async-start | bytes 2097152 | tf_op jit(solution)/shard_map/all_to_all | solution.py:316
  18.0 45.1 %collective-permute-start = (f32[2,2,256,256]{3,2,1,0:T(8,128)}, f32[2,2,256,256]{3,2,1,0:T(8,128)}, u32[]{:S(2)}, u32[]{:S(2)}) collective-permute-start(f32[2,2,256,256]{3,2,1,0:T(8,128)} %dynamic-slice_bitcast_fusion), channel_id=1, source_target_pairs={{0,2},{1,3},{2,0},{3,1},{4,6},{5,7},{6,4},{7,5},{8,10},{9,11},{10,... | collective-permute-start | bytes 3145736 | tf_op jit(solution)/shard_map/ppermute | solution.py:313
  23.8 4.0 %copy-start.2 = (f32[3,2,4,4]{3,2,1,0:T(4,128)S(1)}, f32[3,2,4,4]{3,2,1,0:T(4,128)}, u32[]{:S(2)}) copy-start(f32[3,2,4,4]{3,2,1,0:T(4,128)} %param.7) | copy-start | bytes 1156
  33.5 39.3 %collective-permute-start.1 = (f32[2,2,256,256]{3,2,1,0:T(8,128)}, f32[2,2,256,256]{3,2,1,0:T(8,128)}, u32[]{:S(2)}, u32[]{:S(2)}) collective-permute-start(f32[2,2,256,256]{3,2,1,0:T(8,128)} %bitcast.7), channel_id=1, source_target_pairs={{0,2},{1,3},{2,0},{3,1},{4,6},{5,7},{6,4},{7,5},{8,10},{9,11},{10,... | collective-permute-start | bytes 3145736 | tf_op jit(solution)/shard_map/ppermute | solution.py:313
  33.5 21.4 %all-to-all-start.1 = ((f32[16,2,2,16,256]{4,3,2,1,0:T(8,128)}), f32[16,2,2,16,256]{4,3,2,1,0:T(8,128)S(1)}, u32[]{:S(2)}, u32[]{:S(2)}) async-start(f32[16,2,2,16,256]{4,3,2,1,0:T(8,128)} %merged.8), calls=%async_computation.1 | async-start | bytes 2097152 | tf_op jit(solution)/shard_map/all_to_all | solution.py:316
  44.7 1.0 copy-start.3
  54.9 31.3 %all-to-all-start.3 = ((f32[16,2,4,16,256]{4,3,2,1,0:T(8,128)}), f32[16,2,4,16,256]{4,3,2,1,0:T(8,128)S(1)}, u32[]{:S(2)}, u32[]{:S(2)}) async-start(f32[16,2,4,16,256]{4,3,2,1,0:T(8,128)} %merged.11), calls=%async_computation.3 | async-start | bytes 4194304 | tf_op jit(solution)/shard_map/all_to_all | solution.py:316
  61.1 35.5 %collective-permute-start.3 = (f32[2,2,256,256]{3,2,1,0:T(8,128)}, f32[2,2,256,256]{3,2,1,0:T(8,128)S(1)}, u32[]{:S(2)}, u32[]{:S(2)}) collective-permute-start(f32[2,2,256,256]{3,2,1,0:T(8,128)} %bitcast.11), channel_id=1, source_target_pairs={{0,2},{1,3},{2,0},{3,1},{4,6},{5,7},{6,4},{7,5},{8,10},{9,11},{10,... | collective-permute-start | bytes 3145736 | tf_op jit(solution)/shard_map/ppermute | solution.py:313
  88.8 51.4 %collective-permute-start.4 = (f32[2,4,256,256]{3,2,1,0:T(8,128)}, f32[2,4,256,256]{3,2,1,0:T(8,128)}, u32[]{:S(2)}, u32[]{:S(2)}) collective-permute-start(f32[2,4,256,256]{3,2,1,0:T(8,128)} %bitcast.15), channel_id=1, source_target_pairs={{0,2},{1,3},{2,0},{3,1},{4,6},{5,7},{6,4},{7,5},{8,10},{9,11},{10,... | collective-permute-start | bytes 6291464 | tf_op jit(solution)/shard_map/ppermute | solution.py:313
  90.8 32.8 %all-to-all-start.4 = ((f32[16,2,8,8,256]{4,3,2,1,0:T(8,128)}), f32[16,2,8,8,256]{4,3,2,1,0:T(8,128)S(1)}, u32[]{:S(2)}, u32[]{:S(2)}) async-start(f32[16,2,8,8,256]{4,3,2,1,0:T(8,128)} %get-tuple-element.55), calls=%async_computation.4 | async-start | bytes 4194304 | tf_op jit(solution)/shard_map/all_to_all | solution.py:316
  123.6 1.4 copy-start
  125.0 32.8 %all-to-all-start.2 = ((f32[16,2,8,8,256]{4,3,2,1,0:T(8,128)}), f32[16,2,8,8,256]{4,3,2,1,0:T(8,128)S(1)}, u32[]{:S(2)}, u32[]{:S(2)}) async-start(f32[16,2,8,8,256]{4,3,2,1,0:T(8,128)} %get-tuple-element.51), calls=%async_computation.2 | async-start | bytes 4194304 | tf_op jit(solution)/shard_map/all_to_all | solution.py:316
  130.8 1.6 copy-start.1
  137.6 29.4 %collective-permute-start.7 = (f32[2,4,16,8,256]{4,3,2,1,0:T(8,128)}, f32[2,4,16,8,256]{4,3,2,1,0:T(8,128)S(1)}, u32[]{:S(2)}, u32[]{:S(2)}) collective-permute-start(f32[2,4,16,8,256]{4,3,2,1,0:T(8,128)} %bitcast.21), channel_id=1, source_target_pairs={{0,2},{1,3},{2,0},{3,1},{4,6},{5,7},{6,4},{7,5},{8,10},{9,11},{10,... | collective-permute-start | bytes 3145736 | tf_op jit(solution)/shard_map/ppermute | solution.py:313
  160.9 14.0 %collective-permute-start.6 = (f32[2,4,8,8,256]{4,3,2,1,0:T(8,128)S(1)}, f32[2,4,8,8,256]{4,3,2,1,0:T(8,128)S(1)}, u32[]{:S(2)}, u32[]{:S(2)}) collective-permute-start(f32[2,4,8,8,256]{4,3,2,1,0:T(8,128)S(1)} %bitcast.38), channel_id=1, source_target_pairs={{0,2},{1,3},{2,0},{3,1},{4,6},{5,7},{6,4},{7,5},{8,10},{9,11},{10,... | collective-permute-start | bytes 1572872 | tf_op jit(solution)/shard_map/ppermute | solution.py:313
  165.0 21.1 %collective-permute-start.5 = (f32[2,4,8,8,256]{4,3,2,1,0:T(8,128)S(1)}, f32[2,4,8,8,256]{4,3,2,1,0:T(8,128)S(1)}, u32[]{:S(2)}, u32[]{:S(2)}) collective-permute-start(f32[2,4,8,8,256]{4,3,2,1,0:T(8,128)S(1)} %bitcast.39), channel_id=1, source_target_pairs={{0,2},{1,3},{2,0},{3,1},{4,6},{5,7},{6,4},{7,5},{8,10},{9,11},{10,... | collective-permute-start | bytes 1572872 | tf_op jit(solution)/shard_map/ppermute | solution.py:313

commit v4 on v3

--- a/solution.py
+++ b/solution.py
@@ -270,7 +270,7 @@
         cost_estimate=cost(1),
         compiler_params=params(16),
         name="pair",
-    )(bit, gates, both, both, held.reshape(full))
+    )(bit, gates, hbm(both), hbm(both), held.reshape(full))
     return held, back.reshape(2, CHUNK, 8 * count, 8, G)
 
 
@@ -286,13 +286,13 @@
         out_shape=jax.ShapeDtypeStruct(full, f32),
         grid_spec=pltpu.PrefetchScalarGridSpec(
             num_scalar_prefetch=1,
-            grid=(CHUNK // 2,),
+            grid=(1,),
             in_specs=[
-                pl.BlockSpec((2, 2, wide, 8, G), lambda h, s: (0, h, 0, 0, 0)),
+                pl.BlockSpec((2, CHUNK, wide, 8, G), lambda h, s: (0, h, 0, 0, 0)),
                 pl.BlockSpec(memory_space=pl.ANY),
             ],
             out_specs=pl.BlockSpec(
-                (2, None, 2, wide, 8, G), lambda h, s: (0, 2 * (1 - s[0]), h, first, half, 0)
+                (2, None, CHUNK, wide, 8, G), lambda h, s: (0, 2 * (1 - s[0]), h, first, half, 0)
             ),
         ),
         input_output_aliases={2: 0},

time: 190 us -> 189 us (level)
  local copies, waits for them, and re-layouts: 7.56 us -> 3.69 us
  Pallas kernels: 59.8 us -> 62.6 us
    unnamed x8 -> x2, local copies, waits for them, and re-layouts: 3.9 us -> 0.01 us
    pallas_call x3, Pallas kernels: 11.4 us -> 14.5 us  [pair(): pl.pallas_call(pair_kernel, out_shape=[jax.ShapeDtypeStruct(full, f32), j...]
  transfers between devices with their start and end apart: 13 -> 13, of which waited for: 9 -> 9; matrix products, arithmetic and copies ran while one was open for 1% -> 1% of each run, Pallas kernels for 32% -> 33%
where the time goes in v4:
time: 189 us; the launch traced here: 187 us
  waiting for transfers between devices  80.6 us (43%)
  Pallas kernels  62.6 us (33%)
  starting transfers between devices  39.7 us (21%)
  local copies, waits for them, and re-layouts  3.69 us (2%)
    all_to_all x5, waiting for transfers between devices, remap(): lax.all_to_all(value, 'wide', split_axis=0, concat_axis=0, tiled=True)  51 us
    ppermute x8, waiting for transfers between devices, swapped(): return lax.ppermute(value, 'narrow', partners)  29.6 us
    all_to_all x5, starting transfers between devices, remap(): lax.all_to_all(value, 'wide', split_axis=0, concat_axis=0, tiled=True)  28 us
    pallas_call x6, Pallas kernels, merged(): pl.pallas_call(kernel, out_shape=[out] * parts, grid_spec=pltpu.PrefetchS...  27.5 us
    pallas_call x3, Pallas kernels, pair(): pl.pallas_call(pair_kernel, out_shape=[jax.ShapeDtypeStruct(full, f32), j...  14.5 us
    ppermute x8, starting transfers between devices, swapped(): return lax.ppermute(value, 'narrow', partners)  11.7 us
    pallas_call x2, Pallas kernels, narrow(): pl.pallas_call(kernel, out_shape=jax.ShapeDtypeStruct(full, f32), grid_sp...  11.3 us
    pallas_call x3, Pallas kernels, local(): pl.pallas_call(local_kernel, out_shape=jax.ShapeDtypeStruct((2, count, 2,...  6.55 us
  transfers between devices with their start and end apart: 13, of which 9 were waited for; matrix products, arithmetic and copies ran while one was open for 1% of the time, Pallas kernels for 33%

profile of v4, /device:TPU:1, one launch (start us, length us, event | category | flops | bytes accessed | tf_op | source)
XLA Modules:
  0.0 186.6 jit_solution(9739117649352677953)
XLA Ops:
  0.0 1.3 dynamic-slice_bitcast_fusion.1
  1.3 3.8 %collective-permute-start.2 = (f32[2,2,256,256]{3,2,1,0:T(8,128)S(1)}, f32[2,2,256,256]{3,2,1,0:T(8,128)}, u32[]{:S(2)}, u32[]{:S(2)}) collective-permute-start(f32[2,2,256,256]{3,2,1,0:T(8,128)S(1)} %dynamic-slice_bitcast_fusion.1), channel_id=1, source_target_pairs={{0,2},{1,3},{2,0},{3,1},{4,6},{5,7},{6,4},{7,5},{8,10},{9,11},{10,... | collective-permute-start | bytes 3145736 | tf_op jit(solution)/shard_map/ppermute | solution.py:313
  5.1 3.9 %merged.6 = f32[16,2,2,16,256]{4,3,2,1,0:T(8,128)} custom-call(s32[1]{0:T(128)} %constant.27.clone.1.start_ref, f32[2,16,256,256]{3,2,1,0:T(8,128)} %bitcast.35, f32[2,256,256]{2,1,0:T(8,128)} %low_ref.5, f32[2,256,256]{2,1,0:T(8,128)} %mid_ref.11), custom_call_target="tpu_custom_call" | custom-call | flops 1 | bytes 1 | tf_op jit(solution)/shard_map/merged/pallas_call | solution.py:88
  9.1 6.6 %all-to-all-start = ((f32[16,2,2,16,256]{4,3,2,1,0:T(8,128)}), f32[16,2,2,16,256]{4,3,2,1,0:T(8,128)S(1)}, u32[]{:S(2)}, u32[]{:S(2)}) async-start(f32[16,2,2,16,256]{4,3,2,1,0:T(8,128)} %merged.6), calls=%async_computation | async-start | bytes 2097152 | tf_op jit(solution)/shard_map/all_to_all | solution.py:316
  15.7 2.3 %dynamic-slice_bitcast_fusion = f32[2,2,256,256]{3,2,1,0:T(8,128)} fusion(f32[2,1,1,16,256,256]{5,4,3,2,1,0:T(8,128)} %param.4, s32[]{:T(128)S(6)} %select_n.7), kind=kLoop, calls=%fused_computation | loop fusion | bytes 2097156 | tf_op jit(solution)/shard_map/dynamic_slice | solution.py:323
  18.0 0.1 collective-permute-start
  18.1 5.8 %merged.7 = (f32[16,2,8,8,256]{4,3,2,1,0:T(8,128)}, f32[16,2,8,8,256]{4,3,2,1,0:T(8,128)}) custom-call(s32[1]{0:T(128)S(6)} %mul.12.start_ref, f32[2,16,256,256]{3,2,1,0:T(8,128)} %bitcast.36, f32[2,256,256]{2,1,0:T(8,128)} %low_ref.5, f32[2,256,256]{2,1,0:T(8,128)} %mid_ref.11), custom_call_target="tpu_custom_call" | custom-call | flops 1 | bytes 1 | tf_op jit(solution)/shard_map/merged/pallas_call | solution.py:88
  23.8 0.0 copy-start
  23.8 4.0 %merged.8 = f32[16,2,2,16,256]{4,3,2,1,0:T(8,128)} custom-call(s32[1]{0:T(128)} %constant.31.clone.1.start_ref, f32[2,16,256,256]{3,2,1,0:T(8,128)} %bitcast.37, f32[2,256,256]{2,1,0:T(8,128)} %low_ref.5, f32[2,256,256]{2,1,0:T(8,128)} %mid_ref.11), custom_call_target="tpu_custom_call" | custom-call | flops 1 | bytes 1 | tf_op jit(solution)/shard_map/merged/pallas_call | solution.py:88
  27.8 0.0 copy-done
  27.8 0.1 reshape.75.gate_ref
  27.9 3.6 %all-to-all-done = f32[16,2,2,16,256]{4,3,2,1,0:T(8,128)S(1)} async-done(((f32[16,2,2,16,256]{4,3,2,1,0:T(8,128)}), f32[16,2,2,16,256]{4,3,2,1,0:T(8,128)S(1)}, u32[]{:S(2)}, u32[]{:S(2)}) %all-to-all-start) | async-done | bytes 1048608 | tf_op jit(solution)/shard_map/all_to_all | solution.py:316
  31.5 2.0 %local.3 = f32[2,2,2,2,2,2,16,256]{7,6,5,4,3,2,1,0:T(8,128)} custom-call(f32[96]{0:T(128)S(1)} %reshape.75.gate_ref, f32[2,2,2,2,2,2,16,256]{7,6,5,4,3,2,1,0:T(8,128)S(1)} %bitcast.29), custom_call_target="tpu_custom_call" | custom-call | flops 1 | bytes 1 | tf_op jit(solution)/shard_map/local/pallas_call | solution.py:161
  33.5 0.0 collective-permute-start.1
  33.5 5.6 %all-to-all-start.1 = ((f32[16,2,2,16,256]{4,3,2,1,0:T(8,128)}), f32[16,2,2,16,256]{4,3,2,1,0:T(8,128)S(1)}, u32[]{:S(2)}, u32[]{:S(2)}) async-start(f32[16,2,2,16,256]{4,3,2,1,0:T(8,128)} %merged.8), calls=%async_computation.1 | async-start | bytes 2097152 | tf_op jit(solution)/shard_map/all_to_all | solution.py:316
  39.1 5.7 %merged.11 = f32[16,2,4,16,256]{4,3,2,1,0:T(8,128)} custom-call(s32[1]{0:T(128)} %constant.32.clone.1.start_ref, f32[2,16,256,256]{3,2,1,0:T(8,128)} %bitcast.38, f32[2,256,256]{2,1,0:T(8,128)} %low_ref.5, f32[2,256,256]{2,1,0:T(8,128)} %mid_ref.11), custom_call_target="tpu_custom_call" | custom-call | flops 1 | bytes 1 | tf_op jit(solution)/shard_map/merged/pallas_call | solution.py:88
  44.7 0.0 collective-permute-done.2.x_ref
  44.8 4.1 %merged.9 = (f32[16,2,8,8,256]{4,3,2,1,0:T(8,128)}, f32[16,2,8,8,256]{4,3,2,1,0:T(8,128)}) custom-call(s32[1]{0:T(128)} %constant.25.clone.1.start_ref, f32[2,2,256,256]{3,2,1,0:T(8,128)} %collective-permute-done.2.x_ref, f32[2,256,256]{2,1,0:T(8,128)} %low_ref.5, f32[2,256,256]{2,1,0:T(8,128)} %mid_ref.11, ...), custom_call_target="tpu_custom_call", output_to_operand_aliasing={{0}: (4, {}), {1}: (5, {})} | custom-call | flops 30000001024 | bytes 1 | tf_op jit(solution)/shard_map/merged/pallas_call | solution.py:88
  48.8 6.0 %all-to-all-done.1 = f32[16,2,2,16,256]{4,3,2,1,0:T(8,128)S(1)} async-done(((f32[16,2,2,16,256]{4,3,2,1,0:T(8,128)}), f32[16,2,2,16,256]{4,3,2,1,0:T(8,128)S(1)}, u32[]{:S(2)}, u32[]{:S(2)}) %all-to-all-start.1) | async-done | bytes 1048608 | tf_op jit(solution)/shard_map/all_to_all | solution.py:316
  54.9 4.3 %all-to-all-start.3 = ((f32[16,2,4,16,256]{4,3,2,1,0:T(8,128)}), f32[16,2,4,16,256]{4,3,2,1,0:T(8,128)S(1)}, u32[]{:S(2)}, u32[]{:S(2)}) async-start(f32[16,2,4,16,256]{4,3,2,1,0:T(8,128)} %merged.11), calls=%async_computation.3 | async-start | bytes 4194304 | tf_op jit(solution)/shard_map/all_to_all | solution.py:316
  59.1 1.9 %local.4.refs_1_ = f32[2,2,2,2,2,2,16,256]{7,6,5,4,3,2,1,0:T(8,128)} custom-call(f32[96]{0:T(128)S(1)} %reshape.75.gate_ref, f32[2,2,2,2,2,2,16,256]{7,6,5,4,3,2,1,0:T(8,128)S(1)} %bitcast.30), custom_call_target="tpu_custom_call" | custom-call | flops 1 | bytes 1 | tf_op jit(solution)/shard_map/local/pallas_call | solution.py:161
  61.1 2.0 %collective-permute-start.3 = (f32[2,2,256,256]{3,2,1,0:T(8,128)}, f32[2,2,256,256]{3,2,1,0:T(8,128)}, u32[]{:S(2)}, u32[]{:S(2)}) collective-permute-start(f32[2,2,256,256]{3,2,1,0:T(8,128)} %bitcast.11), channel_id=1, source_target_pairs={{0,2},{1,3},{2,0},{3,1},{4,6},{5,7},{6,4},{7,5},{8,10},{9,11},{10,... | collective-permute-start | bytes 3145736 | tf_op jit(solution)/shard_map/ppermute | solution.py:313
  63.0 0.0 collective-permute-done.x_ref
  63.0 9.7 %collective-permute-done.1 = f32[2,2,256,256]{3,2,1,0:T(8,128)} collective-permute-done((f32[2,2,256,256]{3,2,1,0:T(8,128)}, f32[2,2,256,256]{3,2,1,0:T(8,128)}, u32[]{:S(2)}, u32[]{:S(2)}) %collective-permute-start.1) | collective-permute-done | bytes 1048608 | tf_op jit(solution)/shard_map/ppermute | solution.py:313
  72.8 4.1 %merged.10 = (f32[16,2,8,8,256]{4,3,2,1,0:T(8,128)}, f32[16,2,8,8,256]{4,3,2,1,0:T(8,128)}) custom-call(s32[1]{0:T(128)} %constant.25.clone.1.start_ref, f32[2,2,256,256]{3,2,1,0:T(8,128)} %collective-permute-done.x_ref, f32[2,256,256]{2,1,0:T(8,128)} %low_ref.5, f32[2,256,256]{2,1,0:T(8,128)} %mid_ref.11, ...), custom_call_target="tpu_custom_call", output_to_operand_aliasing={{0}: (4, {}), {1}: (5, {})} | custom-call | flops 30000001024 | bytes 1 | tf_op jit(solution)/shard_map/merged/pallas_call | solution.py:88
  76.9 9.4 %all-to-all-done.3 = f32[16,2,4,16,256]{4,3,2,1,0:T(8,128)S(1)} async-done(((f32[16,2,4,16,256]{4,3,2,1,0:T(8,128)}), f32[16,2,4,16,256]{4,3,2,1,0:T(8,128)S(1)}, u32[]{:S(2)}, u32[]{:S(2)}) %all-to-all-start.3) | async-done | bytes 2097184 | tf_op jit(solution)/shard_map/all_to_all | solution.py:316
  86.3 2.6 %local.5 = f32[2,4,2,2,2,2,16,256]{7,6,5,4,3,2,1,0:T(8,128)} custom-call(f32[96]{0:T(128)S(1)} %reshape.75.gate_ref, f32[2,2,2,2,2,4,16,256]{7,6,5,4,3,2,1,0:T(8,128)S(1)} %bitcast.28), custom_call_target="tpu_custom_call" | custom-call | flops 1 | bytes 1 | tf_op jit(solution)/shard_map/local/pallas_call | solution.py:161
  88.9 1.8 collective-permute-start.4
  90.8 5.8 %all-to-all-start.4 = ((f32[16,2,8,8,256]{4,3,2,1,0:T(8,128)}), f32[16,2,8,8,256]{4,3,2,1,0:T(8,128)}, u32[]{:S(2)}, u32[]{:S(2)}) async-start(f32[16,2,8,8,256]{4,3,2,1,0:T(8,128)} %get-tuple-element.55), calls=%async_computation.4 | async-start | bytes 4194304 | tf_op jit(solution)/shard_map/all_to_all | solution.py:316
  96.6 0.0 collective-permute-done.3
  96.6 5.8 %narrow.2.held_ref = f32[2,4,4,2,2,2,2,16,256]{8,7,6,5,4,3,2,1,0:T(8,128)} custom-call(s32[1]{0:T(128)} %bitcast.bit_ref, f32[96]{0:T(128)S(1)} %reshape.75.gate_ref, f32[2,2,2,2,2,2,16,256]{7,6,5,4,3,2,1,0:T(8,128)} %bitcast.8.refs_0_, f32[2,2,2,2,2,2,16,256]{7,6,5,4,3,2,1,0:T(8,128)} %local.4.refs_1_, f32[2,2,2,2,2,2,16,256]{7,6,5,4,3,2,1,0:T(8,128)} %bitcast.10.refs_2_, ...), custom_call_target="tpu_custom_call" | custom-call | flops 20000000000 | bytes 1 | tf_op jit(solution)/shard_map/narrow/pallas_call | solution.py:209
  102.4 21.2 %all-to-all-done.4 = f32[16,2,8,8,256]{4,3,2,1,0:T(8,128)} async-done(((f32[16,2,8,8,256]{4,3,2,1,0:T(8,128)}), f32[16,2,8,8,256]{4,3,2,1,0:T(8,128)}, u32[]{:S(2)}, u32[]{:S(2)}) %all-to-all-start.4) | async-done | bytes 2097184 | tf_op jit(solution)/shard_map/all_to_all | solution.py:316
  123.6 5.7 %all-to-all-start.2 = ((f32[16,2,8,8,256]{4,3,2,1,0:T(8,128)}), f32[16,2,8,8,256]{4,3,2,1,0:T(8,128)}, u32[]{:S(2)}, u32[]{:S(2)}) async-start(f32[16,2,8,8,256]{4,3,2,1,0:T(8,128)} %get-tuple-element.51), calls=%async_computation.2 | async-start | bytes 4194304 | tf_op jit(solution)/shard_map/all_to_all | solution.py:316
  129.3 6.3 %pair.3 = (f32[2,4,4,2,2,2,2,16,256]{8,7,6,5,4,3,2,1,0:T(8,128)}, f32[2,4,2,2,2,2,8,256]{7,6,5,4,3,2,1,0:T(8,128)}) custom-call(s32[1]{0:T(128)} %bitcast.bit_ref, f32[96]{0:T(128)S(1)} %reshape.75.gate_ref, f32[2,2,2,2,2,2,4,8,256]{8,7,6,5,4,3,2,1,0:T(8,128)} %bitcast.18.own_ref.far_ref, ...), custom_call_target="tpu_custom_call", output_to_operand_aliasing={{0}: (4, {})} | custom-call | flops 1 | bytes 1 | tf_op jit(solution)/shard_map/pair/pallas_call | solution.py:253
  135.7 1.0 collective-permute-start.7
  136.7 3.5 %collective-permute-done.4 = f32[2,4,256,256]{3,2,1,0:T(8,128)S(1)} collective-permute-done((f32[2,4,256,256]{3,2,1,0:T(8,128)}, f32[2,4,256,256]{3,2,1,0:T(8,128)S(1)}, u32[]{:S(2)}, u32[]{:S(2)}) %collective-permute-start.4) | collective-permute-done | bytes 2097184 | tf_op jit(solution)/shard_map/ppermute | solution.py:313
  140.2 5.5 %narrow.3.held_ref = f32[2,4,4,2,2,2,2,16,256]{8,7,6,5,4,3,2,1,0:T(8,128)} custom-call(s32[1]{0:T(128)} %bitcast.bit_ref, f32[96]{0:T(128)S(1)} %reshape.75.gate_ref, f32[2,4,2,2,2,2,16,256]{7,6,5,4,3,2,1,0:T(8,128)} %bitcast.16.refs_0_, f32[2,4,2,2,2,2,16,256]{7,6,5,4,3,2,1,0:T(8,128)S(1)} %bitcast.31, ...), custom_call_target="tpu_custom_call", output_to_operand_aliasing={{}: (4, {})} | custom-call | flops 24999999488 | bytes 1 | tf_op jit(solution)/shard_map/narrow/pallas_call | solution.py:209
  145.7 10.7 %all-to-all-done.2 = f32[16,2,8,8,256]{4,3,2,1,0:T(8,128)} async-done(((f32[16,2,8,8,256]{4,3,2,1,0:T(8,128)}), f32[16,2,8,8,256]{4,3,2,1,0:T(8,128)}, u32[]{:S(2)}, u32[]{:S(2)}) %all-to-all-start.2) | async-done | bytes 2097184 | tf_op jit(solution)/shard_map/all_to_all | solution.py:316
  156.4 4.1 %pair.4 = (f32[2,4,4,2,2,2,2,16,256]{8,7,6,5,4,3,2,1,0:T(8,128)}, f32[2,4,1,2,2,2,8,256]{7,6,5,4,3,2,1,0:T(8,128)S(1)}) custom-call(s32[1]{0:T(128)} %bitcast.bit_ref, f32[96]{0:T(128)S(1)} %reshape.75.gate_ref, f32[2,2,2,2,2,2,4,8,256]{8,7,6,5,4,3,2,1,0:T(8,128)} %bitcast.13.own_ref.far_ref, ...), custom_call_target="tpu_custom_call", output_to_operand_aliasing={{0}: (4, {})} | custom-call | flops 1 | bytes 1 | tf_op jit(solution)/shard_map/pair/pallas_call | solution.py:253
  160.5 1.0 collective-permute-start.6
  161.5 4.1 %pair.5 = (f32[2,4,4,2,2,2,2,16,256]{8,7,6,5,4,3,2,1,0:T(8,128)}, f32[2,4,1,2,2,2,8,256]{7,6,5,4,3,2,1,0:T(8,128)S(1)}) custom-call(s32[1]{0:T(128)} %bitcast.bit_ref, f32[96]{0:T(128)S(1)} %reshape.75.gate_ref, f32[2,2,2,2,2,2,4,8,256]{8,7,6,5,4,3,2,1,0:T(8,128)} %bitcast.13.own_ref.far_ref, ...), custom_call_target="tpu_custom_call", output_to_operand_aliasing={{0}: (4, {})} | custom-call | flops 1 | bytes 1 | tf_op jit(solution)/shard_map/pair/pallas_call | solution.py:253
  165.6 2.0 %collective-permute-start.5 = (f32[2,4,8,8,256]{4,3,2,1,0:T(8,128)S(1)}, f32[2,4,8,8,256]{4,3,2,1,0:T(8,128)S(1)}, u32[]{:S(2)}, u32[]{:S(2)}) collective-permute-start(f32[2,4,8,8,256]{4,3,2,1,0:T(8,128)S(1)} %bitcast.33), channel_id=1, source_target_pairs={{0,2},{1,3},{2,0},{3,1},{4,6},{5,7},{6,4},{7,5},{8,10},{9,11},{10,... | collective-permute-start | bytes 1572872 | tf_op jit(solution)/shard_map/ppermute | solution.py:313
  167.5 0.0 collective-permute-done.7.piece_ref
  167.5 1.0 place.3.held_ref
  168.6 6.0 %collective-permute-done.6.piece_ref = f32[2,4,8,8,256]{4,3,2,1,0:T(8,128)S(1)} collective-permute-done((f32[2,4,8,8,256]{4,3,2,1,0:T(8,128)S(1)}, f32[2,4,8,8,256]{4,3,2,1,0:T(8,128)S(1)}, u32[]{:S(2)}, u32[]{:S(2)}) %collective-permute-start.6) | collective-permute-done | bytes 524320 | tf_op jit(solution)/shard_map/ppermute | solution.py:313
  174.5 0.8 place.4.held_ref
  175.4 10.4 %collective-permute-done.5.piece_ref = f32[2,4,8,8,256]{4,3,2,1,0:T(8,128)S(1)} collective-permute-done((f32[2,4,8,8,256]{4,3,2,1,0:T(8,128)S(1)}, f32[2,4,8,8,256]{4,3,2,1,0:T(8,128)S(1)}, u32[]{:S(2)}, u32[]{:S(2)}) %collective-permute-start.5) | collective-permute-done | bytes 524320 | tf_op jit(solution)/shard_map/ppermute | solution.py:313
  185.8 0.8 place.5
Async XLA Ops:
  1.3 43.4 %collective-permute-start.2 = (f32[2,2,256,256]{3,2,1,0:T(8,128)S(1)}, f32[2,2,256,256]{3,2,1,0:T(8,128)}, u32[]{:S(2)}, u32[]{:S(2)}) collective-permute-start(f32[2,2,256,256]{3,2,1,0:T(8,128)S(1)} %dynamic-slice_bitcast_fusion.1), channel_id=1, source_target_pairs={{0,2},{1,3},{2,0},{3,1},{4,6},{5,7},{6,4},{7,5},{8,10},{9,11},{10,... | collective-permute-start | bytes 3145736 | tf_op jit(solution)/shard_map/ppermute | solution.py:313
  9.1 22.4 %all-to-all-start = ((f32[16,2,2,16,256]{4,3,2,1,0:T(8,128)}), f32[16,2,2,16,256]{4,3,2,1,0:T(8,128)S(1)}, u32[]{:S(2)}, u32[]{:S(2)}) async-start(f32[16,2,2,16,256]{4,3,2,1,0:T(8,128)} %merged.6), calls=%async_computation | async-start | bytes 2097152 | tf_op jit(solution)/shard_map/all_to_all | solution.py:316
  18.0 45.1 %collective-permute-start = (f32[2,2,256,256]{3,2,1,0:T(8,128)}, f32[2,2,256,256]{3,2,1,0:T(8,128)}, u32[]{:S(2)}, u32[]{:S(2)}) collective-permute-start(f32[2,2,256,256]{3,2,1,0:T(8,128)} %dynamic-slice_bitcast_fusion), channel_id=1, source_target_pairs={{0,2},{1,3},{2,0},{3,1},{4,6},{5,7},{6,4},{7,5},{8,10},{9,11},{10,... | collective-permute-start | bytes 3145736 | tf_op jit(solution)/shard_map/ppermute | solution.py:313
  23.8 4.0 %copy-start = (f32[3,2,4,4]{3,2,1,0:T(4,128)S(1)}, f32[3,2,4,4]{3,2,1,0:T(4,128)}, u32[]{:S(2)}) copy-start(f32[3,2,4,4]{3,2,1,0:T(4,128)} %param.7) | copy-start | bytes 1156
  33.5 39.3 %collective-permute-start.1 = (f32[2,2,256,256]{3,2,1,0:T(8,128)}, f32[2,2,256,256]{3,2,1,0:T(8,128)}, u32[]{:S(2)}, u32[]{:S(2)}) collective-permute-start(f32[2,2,256,256]{3,2,1,0:T(8,128)} %bitcast.7), channel_id=1, source_target_pairs={{0,2},{1,3},{2,0},{3,1},{4,6},{5,7},{6,4},{7,5},{8,10},{9,11},{10,... | collective-permute-start | bytes 3145736 | tf_op jit(solution)/shard_map/ppermute | solution.py:313
  33.5 21.4 %all-to-all-start.1 = ((f32[16,2,2,16,256]{4,3,2,1,0:T(8,128)}), f32[16,2,2,16,256]{4,3,2,1,0:T(8,128)S(1)}, u32[]{:S(2)}, u32[]{:S(2)}) async-start(f32[16,2,2,16,256]{4,3,2,1,0:T(8,128)} %merged.8), calls=%async_computation.1 | async-start | bytes 2097152 | tf_op jit(solution)/shard_map/all_to_all | solution.py:316
  54.9 31.4 %all-to-all-start.3 = ((f32[16,2,4,16,256]{4,3,2,1,0:T(8,128)}), f32[16,2,4,16,256]{4,3,2,1,0:T(8,128)S(1)}, u32[]{:S(2)}, u32[]{:S(2)}) async-start(f32[16,2,4,16,256]{4,3,2,1,0:T(8,128)} %merged.11), calls=%async_computation.3 | async-start | bytes 4194304 | tf_op jit(solution)/shard_map/all_to_all | solution.py:316
  61.1 35.5 %collective-permute-start.3 = (f32[2,2,256,256]{3,2,1,0:T(8,128)}, f32[2,2,256,256]{3,2,1,0:T(8,128)}, u32[]{:S(2)}, u32[]{:S(2)}) collective-permute-start(f32[2,2,256,256]{3,2,1,0:T(8,128)} %bitcast.11), channel_id=1, source_target_pairs={{0,2},{1,3},{2,0},{3,1},{4,6},{5,7},{6,4},{7,5},{8,10},{9,11},{10,... | collective-permute-start | bytes 3145736 | tf_op jit(solution)/shard_map/ppermute | solution.py:313
  88.9 51.3 %collective-permute-start.4 = (f32[2,4,256,256]{3,2,1,0:T(8,128)}, f32[2,4,256,256]{3,2,1,0:T(8,128)S(1)}, u32[]{:S(2)}, u32[]{:S(2)}) collective-permute-start(f32[2,4,256,256]{3,2,1,0:T(8,128)} %bitcast.15), channel_id=1, source_target_pairs={{0,2},{1,3},{2,0},{3,1},{4,6},{5,7},{6,4},{7,5},{8,10},{9,11},{10,... | collective-permute-start | bytes 6291464 | tf_op jit(solution)/shard_map/ppermute | solution.py:313
  90.8 32.8 %all-to-all-start.4 = ((f32[16,2,8,8,256]{4,3,2,1,0:T(8,128)}), f32[16,2,8,8,256]{4,3,2,1,0:T(8,128)}, u32[]{:S(2)}, u32[]{:S(2)}) async-start(f32[16,2,8,8,256]{4,3,2,1,0:T(8,128)} %get-tuple-element.55), calls=%async_computation.4 | async-start | bytes 4194304 | tf_op jit(solution)/shard_map/all_to_all | solution.py:316
  123.6 32.8 %all-to-all-start.2 = ((f32[16,2,8,8,256]{4,3,2,1,0:T(8,128)}), f32[16,2,8,8,256]{4,3,2,1,0:T(8,128)}, u32[]{:S(2)}, u32[]{:S(2)}) async-start(f32[16,2,8,8,256]{4,3,2,1,0:T(8,128)} %get-tuple-element.51), calls=%async_computation.2 | async-start | bytes 4194304 | tf_op jit(solution)/shard_map/all_to_all | solution.py:316
  135.7 31.8 %collective-permute-start.7 = (f32[2,4,16,8,256]{4,3,2,1,0:T(8,128)}, f32[2,4,16,8,256]{4,3,2,1,0:T(8,128)S(1)}, u32[]{:S(2)}, u32[]{:S(2)}) collective-permute-start(f32[2,4,16,8,256]{4,3,2,1,0:T(8,128)} %bitcast.21), channel_id=1, source_target_pairs={{0,2},{1,3},{2,0},{3,1},{4,6},{5,7},{6,4},{7,5},{8,10},{9,11},{10,... | collective-permute-start | bytes 3145736 | tf_op jit(solution)/shard_map/ppermute | solution.py:313
  160.5 14.1 %collective-permute-start.6 = (f32[2,4,8,8,256]{4,3,2,1,0:T(8,128)S(1)}, f32[2,4,8,8,256]{4,3,2,1,0:T(8,128)S(1)}, u32[]{:S(2)}, u32[]{:S(2)}) collective-permute-start(f32[2,4,8,8,256]{4,3,2,1,0:T(8,128)S(1)} %bitcast.32), channel_id=1, source_target_pairs={{0,2},{1,3},{2,0},{3,1},{4,6},{5,7},{6,4},{7,5},{8,10},{9,11},{10,... | collective-permute-start | bytes 1572872 | tf_op jit(solution)/shard_map/ppermute | solution.py:313
  165.6 20.2 %collective-permute-start.5 = (f32[2,4,8,8,256]{4,3,2,1,0:T(8,128)S(1)}, f32[2,4,8,8,256]{4,3,2,1,0:T(8,128)S(1)}, u32[]{:S(2)}, u32[]{:S(2)}) collective-permute-start(f32[2,4,8,8,256]{4,3,2,1,0:T(8,128)S(1)} %bitcast.33), channel_id=1, source_target_pairs={{0,2},{1,3},{2,0},{3,1},{4,6},{5,7},{6,4},{7,5},{8,10},{9,11},{10,... | collective-permute-start | bytes 1572872 | tf_op jit(solution)/shard_map/ppermute | solution.py:313
